TPU v7x, 128 devices: a whole 4x4x4 slice. The times are simulated.
128 devices in a mesh: aux: 4 (over y_lo, core), pair: 32 (over z, y_hi, x).
Axes of the slice: x: 4, y: 4 (y_hi: 2, y_lo: 2; y = y_hi * 2 + y_lo), z: 4, core: 2. Of those that a mesh axis runs over, the one named last changes fastest.
Arguments:
- amplitudes: bfloat16 [65536, 512], P('pair', 'aux'), may hold values from -4 to 4
- coulomb: bfloat16 [65536, 512], P('pair'), may hold values from -12 to 12
- df_factors: bfloat16 [65536, 2048], P('pair', 'aux'), may hold values from -0.07861328 to 0.07861328
- thc_left: bfloat16 [512, 1536], P('pair', 'aux'), may hold values from -0.50390625 to 0.50390625
- thc_right: bfloat16 [512, 1536], P('pair', 'aux'), may hold values from -0.50390625 to 0.50390625
- occ_energy: float32 [128], P('pair'), may hold values from -2 to -0.5
- vir_energy: float32 [512], replicated, may hold values from 0.5 to 3
- pivot_energy: float32 [1], replicated, may hold values from -2 to -0.5
Outputs:
- updated: bfloat16 [65536, 512], P('pair', 'aux')
All inputs are finite; a program needn't handle non-finite values.
Results may differ from a plain program's by a relative error of at most 0.0051.
Values may be sent and summed in bfloat16 or wider, within the bound.
A program may use at most 64 MiB of HBM per device.

v0:
```python
import jax
import jax.numpy as jnp
from jax import lax
from jax.sharding import PartitionSpec as P

ITERS = 2


def per_device(
    amplitudes, coulomb, df_factors, thc_left, thc_right, occ_energy, vir_energy, pivot_energy
):
    column_index = lax.axis_index("aux")
    width = amplitudes.shape[1]
    rows = amplitudes.shape[0]
    nvirt = vir_energy.shape[0]
    nocc_local = rows // nvirt
    denom_full = (
        vir_energy[None, :, None]
        + vir_energy[None, None, :]
        - occ_energy[:, None, None]
        - pivot_energy[0]
    ).reshape(rows, nvirt)
    local = amplitudes
    whole = None
    for step in range(ITERS):
        whole = lax.all_gather(local, "aux", axis=1, tiled=True)
        left, right = (
            lax.all_gather(thc_left, "pair", axis=0, tiled=True),
            lax.all_gather(thc_right, "pair", axis=0, tiled=True),
        )
        gram = lax.dot_general(
            df_factors, whole, (((0,), (0,)), ((), ())), preferred_element_type=jnp.float32
        )
        gram = lax.psum(gram, "pair").astype(jnp.bfloat16)
        proj = jnp.dot(whole, right, preferred_element_type=jnp.float32).reshape(
            nocc_local, nvirt, right.shape[1]
        )
        middle = jnp.sum(proj * left.astype(jnp.float32)[None], axis=1)
        weighted = (
            (left.astype(jnp.float32)[None] * middle[:, None, :])
            .astype(jnp.bfloat16)
            .reshape(rows, right.shape[1])
        )
        ladder = lax.dot_general(
            weighted, right, (((1,), (1,)), ((), ())), preferred_element_type=jnp.float32
        )
        cycle = jnp.dot(df_factors, gram, preferred_element_type=jnp.float32)
        part = cycle + ladder
        share = lax.psum_scatter(part, "aux", scatter_dimension=1, tiled=True)
        coulomb_block = lax.dynamic_slice_in_dim(coulomb, column_index * width, width, 1)
        denom_block = lax.dynamic_slice_in_dim(denom_full, column_index * width, width, 1)
        local = ((coulomb_block.astype(jnp.float32) + share) / denom_block).astype(jnp.bfloat16)
        whole = None
    return local


def solution(mesh):
    in_specs = (
        P("pair", "aux"),
        P("pair", None),
        P("pair", "aux"),
        P("pair", "aux"),
        P("pair", "aux"),
        P("pair"),
        P(),
        P(),
    )
    out_specs = P("pair", "aux")
    return jax.shard_map(
        per_device, mesh=mesh, in_specs=in_specs, out_specs=out_specs, check_vma=False
    )
```

profile of v0, /device:TPU:8, one launch (start us, length us, event | category | flops | bytes accessed | tf_op | source)
XLA Modules:
  0.0 725.3 jit_solution(6331696356727031182)
XLA Ops:
  6.5 0.0 copy-start
  6.5 0.0 copy-start.6
  6.5 0.0 all-gather.3.cloned.1.call-start
  6.5 0.7 all-gather.3.cloned.1.call-update
  7.3 0.0 reduce-scatter.3.cloned.1.call-start
  7.3 97.8 %all_gather.15 = bf16[512,384]{1,0:T(8,128)(2,1)S(1)} all-gather(bf16[16,384]{1,0:T(8,128)(2,1)} %param.11), channel_id=1, replica_groups=mesh['aux'=4,'pair'=32] {'pair'}, dimensions={0}, use_global_device_ids=true | all-gather | bytes 405504 | tf_op jit(solution)/shard_map/all_gather | solution.py:28
  105.1 0.1 convert_element_type.38
  105.1 0.0 copy-done.6
  105.1 89.5 %all_gather.16 = bf16[512,384]{1,0:T(8,128)(2,1)S(1)} all-gather(bf16[16,384]{1,0:T(8,128)(2,1)S(1)} %copy-done.6), channel_id=1, replica_groups=mesh['aux'=4,'pair'=32] {'pair'}, dimensions={0}, use_global_device_ids=true | all-gather | bytes 405504 | tf_op jit(solution)/shard_map/all_gather | solution.py:29
  194.6 0.0 all-gather.3.cloned.1.call-done
  194.6 0.0 copy-start.4
  194.6 3.0 multiply_reduce_fusion.1
  197.6 1.5 multiply_convert_fusion.1
  199.1 0.0 copy-done
  199.1 0.0 copy-done.4
  199.1 2.3 fusion.9
  201.4 189.8 %all-reduce.2 = bf16[512,512]{1,0:T(8,128)(2,1)} all-reduce(f32[512,512]{1,0:T(8,128)} %fusion.9), channel_id=1, replica_groups=mesh['aux'=4,'pair'=32] {'pair'}, use_global_device_ids=true, to_apply=%region_0.0 | all-reduce | flops 262144 | bytes 1572864 | tf_op jit(solution)/shard_map/psum | solution.py:34
  391.2 0.0 copy-start.2
  391.2 2.5 fusion.11
  393.6 0.0 copy-done.2
  393.6 3.3 bitcast_add_fusion.1
  397.0 0.0 reduce-scatter.3.cloned.1.call-update
  397.0 0.0 copy-start.7
  397.0 0.0 all-gather.5.cloned.1.call-start
  397.0 1.9 constant_dynamic-slice_fusion
  398.9 2.0 copy.15
  401.0 0.0 copy-done.7
  401.0 0.1 broadcast_add_fusion
  401.1 0.7 sub.27
  401.8 0.0 copy-start.8
  401.8 3.9 copy.17
  405.7 0.0 copy-done.8
  405.7 0.1 broadcast_bitcast_fusion
  406.5 30.2 %reduce-scatter.3.cloned.1.call-done = f32[2048,128]{0,1:T(8,128)} async-done(((f32[2048,512]{0,1:T(8,128)}), f32[2048,128]{0,1:T(8,128)}) %reduce-scatter.3.cloned.1.call-update) | async-done | bytes 1048592 | tf_op jit(solution)/shard_map/reduce_scatter | solution.py:49
  436.6 2.7 fusion.1
  439.4 0.0 all-gather.5.cloned.1.call-update
  439.4 0.0 reduce-scatter.5.cloned.1.call-start
  439.4 29.8 %all-gather.5.cloned.1.call-done = bf16[2048,512]{0,1:T(8,128)(2,1)} async-done(((bf16[2048,128]{0,1:T(8,128)(2,1)}), bf16[2048,512]{0,1:T(8,128)(2,1)}) %all-gather.5.cloned.1.call-update) | async-done | bytes 2097168 | tf_op jit(solution)/shard_map/all_gather | solution.py:26
  469.3 0.0 copy-start.5
  469.3 3.0 multiply_reduce_fusion
  472.3 1.5 multiply_convert_fusion
  473.8 0.0 copy-done.5
  473.8 2.2 convolution_bitcast_fusion
  476.0 195.1 %all-reduce.3 = bf16[512,512]{0,1:T(8,128)(2,1)S(1)} all-reduce(f32[512,512]{0,1:T(8,128)} %convolution_bitcast_fusion), channel_id=1, replica_groups=mesh['aux'=4,'pair'=32] {'pair'}, use_global_device_ids=true, to_apply=%region_3.0 | all-reduce | flops 262144 | bytes 1572864 | tf_op jit(solution)/shard_map/psum | solution.py:34
  671.1 0.0 copy-start.1
  671.1 1.3 fusion.10
  672.4 0.1 copy-done.1
  672.5 3.3 bitcast_add_fusion
  675.8 0.0 copy-start.3
  675.8 0.0 reduce-scatter.5.cloned.1.call-update
  675.9 40.1 %reduce-scatter.5.cloned.1.call-done = f32[2048,128]{0,1:T(8,128)} async-done(((f32[2048,512]{0,1:T(8,128)}), f32[2048,128]{0,1:T(8,128)}) %reduce-scatter.5.cloned.1.call-update) | async-done | bytes 1048592 | tf_op jit(solution)/shard_map/reduce_scatter | solution.py:49
  716.0 0.0 copy-done.3
  716.0 1.8 fusion.3
  717.8 1.0 copy.12
  (1 shorter events, 0.0 us)
Async XLA Ops:
  6.5 192.6 %copy-start = (bf16[2048,512]{1,0:T(8,128)(2,1)S(1)}, bf16[2048,512]{1,0:T(8,128)(2,1)}, u32[]{:S(2)}) copy-start(bf16[2048,512]{1,0:T(8,128)(2,1)} %param.10) | copy-start | bytes 6291460
  6.5 98.6 %copy-start.6 = (bf16[16,384]{1,0:T(8,128)(2,1)S(1)}, bf16[16,384]{1,0:T(8,128)(2,1)}, u32[]{:S(2)}) copy-start(bf16[16,384]{1,0:T(8,128)(2,1)} %param.12) | copy-start | bytes 36868
  6.5 188.1 %all-gather.3.cloned.1.call-start = ((), (), s32[]{:S(2)}) async-start(), calls=%async_computation.2 | async-start | bytes 2621440 | tf_op jit(solution)/shard_map/all_gather | solution.py:26
  7.3 429.4 %reduce-scatter.3.cloned.1.call-start = ((), (), s32[]{:S(2)}) async-start(), calls=%async_computation.3 | async-start | bytes 5242880 | tf_op jit(solution)/shard_map/reduce_scatter | solution.py:49
  194.6 4.5 copy-start.4
  391.2 2.5 copy-start.2
  397.0 4.0 copy-start.7
  397.0 72.3 %all-gather.5.cloned.1.call-start = ((), (), s32[]{:S(2)}) async-start(), calls=%async_computation.4 | async-start | bytes 2621440 | tf_op jit(solution)/shard_map/all_gather | solution.py:26
  401.8 3.9 copy-start.8
  439.4 276.6 %reduce-scatter.5.cloned.1.call-start = ((), (), s32[]{:S(2)}) async-start(), calls=%async_computation.5 | async-start | bytes 5242880 | tf_op jit(solution)/shard_map/reduce_scatter | solution.py:49
  469.3 4.5 copy-start.5
  671.1 1.4 copy-start.1
  675.8 40.1 %copy-start.3 = (bf16[2048,128]{0,1:T(8,128)(2,1)S(1)}, bf16[2048,128]{0,1:T(8,128)(2,1)}, u32[]{:S(2)}) copy-start(bf16[2048,128]{0,1:T(8,128)(2,1)} %copy.15) | copy-start | bytes 1572868
Sparse Core Ops, SparseCore 0:
  9.0 30.6 all-gather.2
  397.1 39.4 reduce-scatter.2
  439.5 29.6 all-gather.4
  676.0 39.9 reduce-scatter.4
where the time goes:
time: 728 us; the launch traced here: 725 us
  blocking collectives  572 us (79%)
  waiting for transfers between devices  101 us (14%)
  matrix products  20.9 us (3%)
  between operations  13.9 us (2%)
  local copies, waits for them, and re-layouts  9.74 us (1%)
  other arithmetic  7.65 us (1%)
    psum x2, blocking collectives, per_device(): gram = lax.psum(gram, 'pair').astype(jnp.bfloat16)  385 us
    all_gather x1, blocking collectives, per_device(): lax.all_gather(thc_left, 'pair', axis=0, tiled=True)  97.8 us
    all_gather x1, blocking collectives, per_device(): lax.all_gather(thc_right, 'pair', axis=0, tiled=True)  89.5 us
    reduce_scatter x2, waiting for transfers between devices, per_device(): share = lax.psum_scatter(part, 'aux', scatter_dimension=1, tiled=True)  70.3 us
    all_gather x2, waiting for transfers between devices, per_device(): whole = lax.all_gather(local, 'aux', axis=1, tiled=True)  29.8 us
  transfers between devices with their start and end apart: 4, of which 3 were waited for; matrix products, arithmetic and copies ran while one was open for 1% of the time, Pallas kernels for 0%

commit v1 on v0

v1 whole, which is shorter than its diff:
```python
import jax
import jax.numpy as jnp
from jax import lax
from jax.experimental import pallas as pl
from jax.experimental.pallas import tpu as pltpu
from jax.sharding import PartitionSpec as P

MESH = pl.DeviceIdType.MESH
BF = jnp.bfloat16
F32 = jnp.float32
N_SEM = 256
N_CHUNK = 8
TN = (((0,), (0,)), ((), ()))
NT = (((1,), (1,)), ((), ()))


def kernel(
    amps, coul, df, tl, tr, occ, vir, piv, out,
    BQ, BR, T0, T1, TS, C, LAD, VA, WB, MID,
    GP1, RA1, CB1, RB1, PB1, RY1, G1,
    GP2, RA2, CB2, RB2, PB2, RY2, G2,
    ss, rs, ls,
):
    a = lax.axis_index("aux")
    p = lax.axis_index("pair")
    Y, c = a // 2, a % 2
    z, yh, x = p // 8, (p // 4) % 2, p % 4
    oY, oc, oyh = 1 - Y, 1 - c, 1 - yh

    def dev(Y=Y, c=c, z=z, yh=yh, x=x):
        return {"aux": Y * 2 + c, "pair": z * 8 + yh * 4 + x}

    ypeers = [dev(Y=oY), dev(yh=oyh), dev(Y=oY, yh=oyh)]
    xpeers = [dev(x=(x + k) % 4) for k in (1, 2, 3)]
    zpeers = [dev(z=(z + k) % 4) for k in (1, 2, 3)]
    core = dev(c=oc)
    rows = pl.multiple_of(Y * 1024, 1024)
    orows = pl.multiple_of(oY * 1024, 1024)

    count = [0]
    started = []

    def send(src, dst, to):
        n = count[0]
        count[0] += 1
        assert n < N_SEM
        copy = pltpu.make_async_remote_copy(
            src_ref=src, dst_ref=dst, send_sem=ss.at[n], recv_sem=rs.at[n],
            device_id=to, device_id_type=MESH,
        )
        copy.start()
        started.append(copy)
        return copy

    def arrive(copies):
        for copy in copies:
            copy.wait_recv()

    locals_ = [
        (df, BQ.at[c]),
        (amps, T0.at[Y]),
        (tl, WB.at[c, Y, 0, z, yh, x]),
        (tr, WB.at[c, Y, 1, z, yh, x]),
        (coul.at[pl.ds(rows, 1024), pl.ds(pl.multiple_of(c * 128, 128), 128)], C.at[0]),
        (coul.at[pl.ds(rows, 1024), pl.ds(pl.multiple_of((2 + c) * 128, 128), 128)], C.at[1]),
    ]
    lcopies = []
    for n, (src, dst) in enumerate(locals_):
        copy = pltpu.make_async_copy(src, dst, ls.at[n])
        copy.start()
        lcopies.append(copy)

    barrier = pltpu.get_barrier_semaphore()
    for to in ypeers + xpeers + zpeers + [core]:
        pl.semaphore_signal(barrier, inc=1, device_id=to, device_id_type=MESH)
    pl.semaphore_wait(barrier, 10)

    thc_y = []
    for to in ypeers:
        thc_y.append(send(tl, WB.at[c, Y, 0, z, yh, x], to))
        thc_y.append(send(tr, WB.at[c, Y, 1, z, yh, x], to))
    t_in = send(amps, T0.at[Y], ypeers[0])
    b_in = send(df, BQ.at[c], core)
    size = 1024 // N_CHUNK

    def move(n):
        return send(
            df.at[pl.ds(pl.multiple_of(oY * 1024 + n * size, size), size), :],
            BR.at[c, pl.ds(n * size, size), :],
            ypeers[0],
        )

    def forward(n):
        block = BR.at[c, pl.ds(n * size, size), :]
        return send(block, block, core)

    moved = [move(n) for n in range(N_CHUNK // 2)]

    def gram_tiles(get, tsrc, put):
        def body(q, _):
            qs = pl.multiple_of(q * 256, 256)
            put(qs, lax.dot_general(get(qs), tsrc, TN, preferred_element_type=F32).astype(BF))
            return 0

        lax.fori_loop(0, 2, body, 0)

    def gram1(f, s, cc):
        def get(qs):
            return BQ[cc, :, pl.ds(qs, 256)]

        def put(qs, value):
            GP1[f, 0, pl.ds(pl.multiple_of(cc * 512 + qs, 256), 256), :] = value

        gram_tiles(get, T0[s], put)

    def gram2(s):
        for cc in range(2):
            def put_own(qs, value):
                GP2[s, Y, pl.ds(pl.multiple_of(cc * 512 + qs, 256), 256), :] = value

            def put_other(qs, value):
                GP2[s, oY, pl.ds(pl.multiple_of(cc * 512 + qs, 256), 256), :] = value

            gram_tiles(lambda qs: BQ[cc, pl.ds(rows, 1024), pl.ds(qs, 256)], T1[s], put_own)
            gram_tiles(lambda qs: BR[cc, :, pl.ds(qs, 256)], T1[s], put_other)

    class Reduce:
        def __init__(self, GP, RA, CB, RB, PB, RY, G, split):
            self.refs = GP, RA, CB, RB, PB, RY, G
            self.split = split
            self.live = {}

        def axes(self, h):
            return (x, xpeers, z, zpeers) if h == 0 else (z, zpeers, x, xpeers)

        def a_start(self, u, h):
            GP, RA = self.refs[:2]
            i, peers, _, _ = self.axes(h)
            self.live["a", u, h] = [
                send(
                    GP.at[u, :, pl.ds(pl.multiple_of(h * 512 + (i + k) % 4 * 128, 128), 128), :],
                    RA.at[u, h, k - 1], peers[k - 1],
                )
                for k in (1, 2, 3)
            ]

        def a_finish(self, u, h):
            GP, RA, CB = self.refs[:3]
            i, _, _, _ = self.axes(h)
            arrive(self.live["a", u, h])
            total = GP[u, :, pl.ds(pl.multiple_of(h * 512 + i * 128, 128), 128), :].astype(F32)
            for k in range(3):
                total = total + RA[u, h, k].astype(F32)
            CB[u, h] = total.astype(BF)

        def b_start(self, u, h):
            CB, RB = self.refs[2:4]
            _, _, j, peers = self.axes(h)
            self.live["b", u, h] = [
                send(
                    CB.at[u, h, :, pl.ds(pl.multiple_of((j + k) % 4 * 32, 32), 32), :],
                    RB.at[u, h, k - 1], peers[k - 1],
                )
                for k in (1, 2, 3)
            ]

        def b_finish(self, u, h, s):
            CB, RB, PB = self.refs[2:5]
            _, _, j, _ = self.axes(h)
            arrive(self.live["b", u, h])
            total = CB[u, h, :, pl.ds(pl.multiple_of(j * 32, 32), 32), :].astype(F32)
            for k in range(3):
                total = total + RB[u, h, k].astype(F32)
            PB[s, h] = total.astype(BF)

        def y_start(self, s, h):
            PB, RY = self.refs[4:6]
            self.live["y", s, h] = [
                send(PB.at[s, h], RY.at[s, h, k], ypeers[k]) for k in range(3)
            ]

        def place(self, s, h):
            G = self.refs[6]
            i, _, j, _ = self.axes(h)
            return G.at[s, :, pl.ds(pl.multiple_of(h * 512 + i * 128 + j * 32, 32), 32), :]

        def y_finish(self, s, h):
            PB, RY, G = self.refs[4:7]
            arrive(self.live["y", s, h])
            i, _, j, _ = self.axes(h)
            at = pl.ds(pl.multiple_of(h * 512 + i * 128 + j * 32, 32), 32)
            got = [RY[s, h, k].astype(F32) for k in range(3)]
            own = PB[s, h].astype(F32)
            if self.split:
                G[s, Y, at, :] = (own + got[1])[0].astype(BF)
                G[s, oY, at, :] = (got[0] + got[2])[0].astype(BF)
            else:
                G[s, :, at, :] = (own + got[0] + (got[1] + got[2])).astype(BF)

        def gb_start(self, s, h):
            _, _, _, peers = self.axes(h)
            at = self.place(s, h)
            self.live["gb", s, h] = [send(at, at, to) for to in peers]

        def gb_finish(self, s, h):
            arrive(self.live["gb", s, h])

        def ga_start(self, s, h):
            G = self.refs[6]
            i, peers, _, _ = self.axes(h)
            at = G.at[s, :, pl.ds(pl.multiple_of(h * 512 + i * 128, 128), 128), :]
            self.live["ga", s, h] = [send(at, at, to) for to in peers]

        def ga_finish(self, s, h):
            arrive(self.live["ga", s, h])

    first = Reduce(GP1, RA1, CB1, RB1, PB1, RY1, G1, True)
    second = Reduce(GP2, RA2, CB2, RB2, PB2, RY2, G2, False)

    def left(cc, yy, start, n):
        return WB[cc, yy, 0, pl.ds(start, n)].reshape(n * 128, 384)

    def right(cc, yy, s):
        return WB[cc, yy, 1, 2 * s + c].reshape(128, 384)

    def middle(it, get):
        MID[it, 0] = jnp.zeros((8, 1536), F32)

        def body(pb, _):
            cc, yy = pb % 2, pb // 2
            r0, r1 = right(cc, yy, 0), right(cc, yy, 1)
            lanes = pl.ds(pl.multiple_of(pb * 384, 128), 384)
            for i in range(2):
                total = jnp.zeros((1, 384), F32)
                for h in range(2):
                    proj = jnp.dot(get(0, i * 512 + h * 256), r0, preferred_element_type=F32)
                    proj = proj + jnp.dot(get(1, i * 512 + h * 256), r1, preferred_element_type=F32)
                    lf = left(cc, yy, 2 * h, 2).astype(F32)
                    total = total + jnp.sum(proj * lf, axis=0, keepdims=True)
                MID[it, 0, pl.ds(i, 1), lanes] = total
            return 0

        lax.fori_loop(0, 4, body, 0)
        return send(MID.at[it, 0], MID.at[it, 1], core)

    def ladder(it, copy):
        copy.wait_recv()

        for pb in range(4):
            cc, yy = pb % 2, pb // 2
            lanes = pl.ds(pb * 384, 384)

            def body(i, _):
                mid = MID[it, 0, pl.ds(i, 1), lanes] + MID[it, 1, pl.ds(i, 1), lanes]
                lf = left(cc, yy, 0, 4)
                at = pl.ds(pl.multiple_of(i * 512, 512), 512)
                for s in range(2):
                    wr = (right(cc, yy, s).astype(F32) * mid).astype(BF)
                    term = lax.dot_general(lf, wr, NT, preferred_element_type=F32)
                    if pb == 0:
                        LAD[s, at, :] = term
                    else:
                        LAD[s, at, :] = LAD[s, at, :] + term
                return 0

            lax.fori_loop(0, 2, body, 0)

    def update(G, s, put):
        def body(n, _):
            at = pl.multiple_of(n * 256, 256)
            here = pl.ds(at, 256)
            mine = pl.ds(pl.multiple_of(Y * 1024 + at, 256), 256)
            total = None
            for cc in range(2):
                q = pl.ds(cc * 512, 512)
                term = jnp.dot(BQ[cc, mine, :], G[s, Y, q, :], preferred_element_type=F32)
                total = term if total is None else total + term
            for cc in range(2):
                q = pl.ds(cc * 512, 512)
                total = total + jnp.dot(BR[cc, here, :], G[s, oY, q, :], preferred_element_type=F32)
            total = total + LAD[s, here, :]
            va = VA[pl.ds(pl.multiple_of(n % 2 * 256, 256), 256), :]
            vb = vir[0:1, pl.ds(pl.multiple_of((2 * s + c) * 128, 128), 128)]
            denom = va + vb - occ[2 * Y + n // 2] - piv[0]
            put(here, ((C[s, here, :].astype(F32) + total) / denom).astype(BF))
            return 0

        lax.fori_loop(0, 4, body, 0)

    halves = (0, 1)
    units = [(s, h) for s in range(2) for h in halves]

    for copy in lcopies:
        copy.wait()
    gram1(0, Y, c)
    for q in range(4):
        row = vir[0:1, q * 128:(q + 1) * 128]
        VA[q * 128:(q + 1) * 128, :] = jnp.transpose(jnp.broadcast_to(row, (128, 128)))
    arrive([b_in])
    gram1(0, Y, oc)
    for h in halves:
        first.a_start(0, h)
    arrive(thc_y)
    lx = [send(WB.at[c, :, 0, z, :, x], WB.at[c, :, 0, z, :, x], to) for to in xpeers]
    rz = [send(WB.at[c, :, 1, z, :, x], WB.at[c, :, 1, z, :, x], to) for to in zpeers]
    for h in halves:
        first.a_finish(0, h)
        first.b_start(0, h)
    arrive(lx)
    lz = [send(WB.at[c, :, 0, z], WB.at[c, :, 0, z], to) for to in zpeers]
    arrive(rz)
    rx = [send(WB.at[c, :, 1, :, :, x], WB.at[c, :, 1, :, :, x], to) for to in xpeers]
    for h in halves:
        first.b_finish(0, h, Y)
    arrive([t_in])
    gram1(1, oY, c)
    gram1(1, oY, oc)
    for h in halves:
        first.a_start(1, h)
    arrive(lz)
    arrive(rx)
    thc_core = [send(WB.at[c, :, 0], WB.at[c, :, 0], core)]
    for k in range(2):
        at = WB.at[c, :, 1, oc + 2 * k]
        thc_core.append(send(at, at, core))
    for h in halves:
        first.a_finish(1, h)
        first.b_start(1, h)
    arrive(thc_core)
    for h in halves:
        first.b_finish(1, h, oY)
    for s, h in units:
        first.y_start(s, h)
    moved += [move(n) for n in range(N_CHUNK // 2, N_CHUNK)]
    mid_copy = middle(0, lambda s, at: T0[s, pl.ds(pl.multiple_of(rows + at, 256), 256), :])
    for s, h in units:
        first.y_finish(s, h)
        first.gb_start(s, h)
    forwarded = []
    for n in range(N_CHUNK // 2):
        arrive([moved[n]])
        forwarded.append(forward(n))
    for s, h in units:
        first.gb_finish(s, h)
        first.ga_start(s, h)
    ladder(0, mid_copy)
    for n in range(N_CHUNK // 2, N_CHUNK):
        arrive([moved[n]])
        forwarded.append(forward(n))
    arrive(forwarded)

    for s in range(2):
        for h in halves:
            first.ga_finish(s, h)

        def put(here, value):
            T1[s, here, :] = value

        update(G1, s, put)
        gram2(s)
        for h in halves:
            second.a_start(s, h)

    mid_copy = middle(1, lambda s, at: T1[s, pl.ds(at, 256), :])
    for s, h in units:
        second.a_finish(s, h)
        second.b_start(s, h)
    for s, h in units:
        second.b_finish(s, h, s)
        second.y_start(s, h)
    ladder(1, mid_copy)
    for s, h in units:
        second.y_finish(s, h)
        second.gb_start(s, h)
    for s, h in units:
        second.gb_finish(s, h)
        second.ga_start(s, h)
    for s in range(2):
        for h in halves:
            second.ga_finish(s, h)

        def put(here, value):
            TS[s, here, :] = value

        update(G2, s, put)
    last = send(TS.at[oY], out.at[pl.ds(rows, 1024), :], ypeers[0])
    out[pl.ds(rows, 1024), :] = TS[Y]
    last.wait_recv()
    for copy in started:
        copy.wait_send()


def per_device(amplitudes, coulomb, df_factors, thc_left, thc_right, occ, vir, pivot):
    any_ = pl.BlockSpec(memory_space=pl.ANY)
    smem = pl.BlockSpec(memory_space=pltpu.SMEM)
    vmem = pl.BlockSpec(memory_space=pltpu.VMEM)

    def reduce_scratch(m):
        return [
            pltpu.VMEM((2, m, 1024, 128), BF),
            pltpu.VMEM((2, 2, 3, m, 128, 128), BF),
            pltpu.VMEM((2, 2, m, 128, 128), BF),
            pltpu.VMEM((2, 2, 3, m, 32, 128), BF),
            pltpu.VMEM((2, 2, m, 32, 128), BF),
            pltpu.VMEM((2, 2, 3, m, 32, 128), BF),
            pltpu.VMEM((2, 2, 1024, 128), BF),
        ]

    return pl.pallas_call(
        kernel,
        out_shape=jax.ShapeDtypeStruct((2048, 128), BF),
        in_specs=[any_] * 5 + [smem, vmem, smem],
        out_specs=vmem,
        scratch_shapes=[
            pltpu.VMEM((2, 2048, 512), BF),
            pltpu.VMEM((2, 1024, 512), BF),
            pltpu.VMEM((2, 2048, 128), BF),
            pltpu.VMEM((2, 1024, 128), BF),
            pltpu.VMEM((2, 1024, 128), BF),
            pltpu.VMEM((2, 1024, 128), BF),
            pltpu.VMEM((2, 1024, 128), F32),
            pltpu.VMEM((512, 128), F32),
            pltpu.VMEM((2, 2, 2, 4, 2, 4, 16, 384), BF),
            pltpu.VMEM((2, 2, 8, 1536), F32),
        ]
        + reduce_scratch(1)
        + reduce_scratch(2)
        + [
            pltpu.SemaphoreType.DMA((N_SEM,)),
            pltpu.SemaphoreType.DMA((N_SEM,)),
            pltpu.SemaphoreType.DMA((6,)),
        ],
        compiler_params=pltpu.CompilerParams(
            collective_id=0, has_side_effects=True, vmem_limit_bytes=56 * 2**20
        ),
    )(amplitudes, coulomb, df_factors, thc_left, thc_right, occ, vir.reshape(1, 512), pivot)


def solution(mesh):
    in_specs = (
        P("pair", "aux"),
        P("pair", None),
        P("pair", "aux"),
        P("pair", "aux"),
        P("pair", "aux"),
        P("pair"),
        P(),
        P(),
    )
    return jax.shard_map(
        per_device, mesh=mesh, in_specs=in_specs, out_specs=P("pair", "aux"), check_vma=False
    )
```

time: 728 us -> 97.8 us (0.13)
  blocking collectives: 572 us -> 0 us
  waiting for transfers between devices: 101 us -> 0 us
  Pallas kernels: 0 us -> 93.7 us
  matrix products: 20.9 us -> 0 us
  between operations: 13.9 us -> 0.66 us
  local copies, waits for them, and re-layouts: 9.74 us -> 1.87 us
  other arithmetic: 7.65 us -> 0 us
    psum x2 -> x0, blocking collectives: 385 us -> none  [per_device(): gram = lax.psum(gram, 'pair').astype(jnp.bfloat16)]
    all_gather x2 -> x0, blocking collectives: 187 us -> none  [the longest x1 97.8 us: per_device(): lax.all_gather(thc_left, 'pair', axis=0, tiled=True)]
    pallas_call x0 -> x1, Pallas kernels: none -> 93.7 us  [per_device(): pl.pallas_call(kernel, out_shape=jax.ShapeDtypeStruct((2048, 128), BF), i...]
    reduce_scatter x2 -> x0, waiting for transfers between devices: 70.3 us -> none  [per_device(): share = lax.psum_scatter(part, 'aux', scatter_dimension=1, tiled=True)]
    all_gather x2 -> x0, waiting for transfers between devices: 29.8 us -> none  [per_device(): whole = lax.all_gather(local, 'aux', axis=1, tiled=True)]
    dot_general x8 -> x0, matrix products: 20.9 us -> none  [the longest x2 6.62 us: per_device(): lax.dot_general(weighted, right, (((1,), (1,)), ((), ())), preferred_elem...]
    convert_element_type x5 -> x0, other arithmetic: 7.52 us -> none  [the longest x2 4.51 us: per_device(): ((coulomb_block.astype(jnp.float32) + share) / denom_block).astype(jnp.bf...]
  transfers between devices with their start and end apart: 4 -> 0, of which waited for: 3 -> 0; matrix products, arithmetic and copies ran while one was open for 1% -> 0% of each run, Pallas kernels for 0% -> 0%
where the time goes in v1:
time: 97.8 us; the launch traced here: 96.3 us
  Pallas kernels  93.7 us (96%)
  local copies, waits for them, and re-layouts  1.87 us (2%)
    pallas_call x1, Pallas kernels, per_device(): pl.pallas_call(kernel, out_shape=jax.ShapeDtypeStruct((2048, 128), BF), i...  93.7 us

profile of v1, /device:TPU:8, one launch (start us, length us, event | category | flops | bytes accessed | tf_op | source)
XLA Modules:
  0.0 96.3 jit_solution(9518296006803633211)
XLA Ops:
  0.7 93.7 %shard_map.82 = bf16[2048,128]{1,0:T(8,128)(2,1)} custom-call(bf16[2048,128]{1,0:T(8,128)(2,1)} %amps.1, bf16[2048,512]{1,0:T(8,128)(2,1)} %coul.1, bf16[2048,512]{1,0:T(8,128)(2,1)} %df.1, bf16[16,384]{1,0:T(8,128)(2,1)} %tl.1, bf16[16,384]{1,0:T(8,128)(2,1)} %tr.1, f32[4]{0:T(128)} %occ.1, f32[1,512]{1,0:T(1,128)} %bitcast.1, f32[1]{0:T(128)S(6)} %copy.10.piv), custom_call_target="tpu_custom_call" | custom-call | tf_op jit(solution)/shard_map/pallas_call | solution.py:409
  94.4 1.9 %copy.11 = bf16[2048,128]{1,0:T(8,128)(2,1)} copy(bf16[2048,128]{1,0:T(8,128)(2,1)} %shard_map.82) | data formatting | bytes 1048576

commit v2 on v0

v2 whole, which is shorter than its diff:
```python
import jax
import jax.numpy as jnp
from jax import lax
from jax.experimental import pallas as pl
from jax.experimental.pallas import tpu as pltpu
from jax.sharding import PartitionSpec as P

MESH = pl.DeviceIdType.MESH
BF = jnp.bfloat16
F32 = jnp.float32
N_SEM = 51
N_MOVE = 8
EARLY = 3
NT = (((1,), (1,)), ((), ()))


def mult(value, n):
    return pl.multiple_of(value, n)


def kernel(
    amps, coul, df, tl, tr, occ, vir, piv, out,
    BQ, BR, T0, TT0, TT1, TS, C, LAD, VA, WB, WR, MID,
    GF1, GP1, RA1, CB1, CF1, RB1, PB1, PF1, RY1, G1,
    GF2, GP2, RA2, CB2, CF2, RB2, PB2, PF2, RY2, G2,
    ss, rs, ls,
):
    a = lax.axis_index("aux")
    p = lax.axis_index("pair")
    Y, c = a // 2, a % 2
    z, yh, x = p // 8, (p // 4) % 2, p % 4
    oY, oc, oyh = 1 - Y, 1 - c, 1 - yh

    def dev(Y=Y, c=c, z=z, yh=yh, x=x):
        return {"aux": Y * 2 + c, "pair": z * 8 + yh * 4 + x}

    ypeers = [dev(Y=oY), dev(yh=oyh), dev(Y=oY, yh=oyh)]
    xpeers = [dev(x=(x + k) % 4) for k in (1, 2, 3)]
    zpeers = [dev(z=(z + k) % 4) for k in (1, 2, 3)]
    core = dev(c=oc)
    rows = mult(Y * 1024, 1024)
    orows = mult(oY * 1024, 1024)

    count = [0]
    groups = []

    class Group:
        def __init__(self, ruler):
            self.n, self.ruler = count[0], ruler
            count[0] += 1
            assert self.n < N_SEM
            groups.append(self)

        def send(self, src, dst, to):
            pltpu.make_async_remote_copy(
                src_ref=src, dst_ref=dst, send_sem=ss.at[self.n], recv_sem=rs.at[self.n],
                device_id=to, device_id_type=MESH,
            ).start()

        def arrive(self):
            pltpu.make_async_copy(self.ruler, self.ruler, rs.at[self.n]).wait()

        def sent(self):
            pltpu.make_async_copy(self.ruler, self.ruler, ss.at[self.n]).wait()

    def one(src, dst, to):
        group = Group(dst)
        group.send(src, dst, to)
        return group

    def to_all(src, dst, peers, ruler):
        group = Group(ruler)
        for to in peers:
            group.send(src, dst, to)
        return group

    piece = pl.ds(mult(c * 768 + Y * 384, 128), 384)
    plane = pl.ds(mult(c * 768, 128), 768)
    lcopies = []
    for n, (src, dst) in enumerate([
        (amps, T0.at[Y]),
        (df, BQ.at[c]),
        (tl, WB.at[0, z, yh, x, :, piece]),
        (tr, WB.at[1, z, yh, x, :, piece]),
        (coul.at[pl.ds(rows, 1024), pl.ds(mult(c * 128, 128), 128)], C.at[0]),
        (coul.at[pl.ds(rows, 1024), pl.ds(mult((2 + c) * 128, 128), 128)], C.at[1]),
    ]):
        copy = pltpu.make_async_copy(src, dst, ls.at[n])
        copy.start()
        lcopies.append(copy)

    barrier = pltpu.get_barrier_semaphore()
    for to in ypeers + xpeers + zpeers + [core]:
        pl.semaphore_signal(barrier, inc=1, device_id=to, device_id_type=MESH)

    def transpose0(s, half):
        for n in range(2):
            at = pl.ds(half * 1024 + n * 512, 512)
            TT0[s, :, at] = jnp.transpose(T0[s, at, :])

    def gram1(f, s, cc, half):
        at = pl.ds(half * 1024, 1024)
        got = jnp.dot(TT0[s, :, at], BQ[cc, at, :], preferred_element_type=F32)
        for q in range(4):
            value = got[:, q * 128:(q + 1) * 128]
            if half == 1:
                value = GF1[f, 0, cc * 4 + q] + value
                GP1[f, 0, cc * 4 + q] = value.astype(BF)
            GF1[f, 0, cc * 4 + q] = value

    lcopies[0].wait()
    transpose0(Y, 0)
    transpose0(Y, 1)
    for q in range(4):
        row = vir[0:1, q * 128:(q + 1) * 128]
        VA[q * 128:(q + 1) * 128, :] = jnp.transpose(jnp.broadcast_to(row, (128, 128)))
    lcopies[1].wait()
    gram1(0, Y, c, 0)
    gram1(0, Y, c, 1)
    pl.semaphore_wait(barrier, 10)

    b_in = one(df, BQ.at[c], core)
    thc_y = Group(WB.at[0, 0, 0, pl.ds(0, 2), :, pl.ds(0, 1152)])
    for to in ypeers:
        thc_y.send(tl, WB.at[0, z, yh, x, :, piece], to)
        thc_y.send(tr, WB.at[1, z, yh, x, :, piece], to)
    t_in = []
    for half in range(2):
        at = pl.ds(half * 1024, 1024)
        t_in.append(one(amps.at[at, :], T0.at[Y, at, :], ypeers[0]))
    size = 1024 // N_MOVE
    moved = []

    def move(count):
        for n in range(len(moved), len(moved) + count):
            src = df.at[pl.ds(mult(oY * 1024 + n * size, size), size), :]
            dst = BR.at[c, pl.ds(n * size, size), :]
            group = Group(BR.at[0, pl.ds(n * size, size), :])
            group.send(src, dst, ypeers[0])
            moved.append(group)

    forwarded = []

    def forward(count):
        start = len(forwarded) * 2
        for n in range(start, start + count * 2, 2):
            moved[n].arrive()
            moved[n + 1].arrive()
            block = BR.at[c, pl.ds(n * size, 2 * size), :]
            forwarded.append(one(block, block, core))

    class Reduce:
        def __init__(self, refs, split):
            self.GF, self.GP, self.RA, self.CB, self.CF = refs[:5]
            self.RB, self.PB, self.PF, self.RY, self.G = refs[5:]
            self.split = split
            self.live = {}

        def axes(self, h):
            return (x, xpeers, z, zpeers) if h == 0 else (z, zpeers, x, xpeers)

        def a_start(self, u, h):
            i, peers, _, _ = self.axes(h)
            group = self.live["a", u, h] = Group(self.RA.at[u, h])
            for k in (1, 2, 3):
                src = self.GP.at[u, :, h * 4 + (i + k) % 4]
                group.send(src, self.RA.at[u, h, k - 1], peers[k - 1])

        def a_finish(self, u):
            group = self.live["b", u] = Group(self.RB.at[u])
            for h in range(2):
                self.live["a", u, h].arrive()
                i, _, j, peers = self.axes(h)
                total = self.GF[u, :, h * 4 + i]
                for k in range(3):
                    total = total + self.RA[u, h, k].astype(F32)
                self.CF[u, h] = total
                self.CB[u, h] = total.astype(BF)
                for k in (1, 2, 3):
                    src = self.CB.at[u, h, :, pl.ds(mult((j + k) % 4 * 32, 32), 32), :]
                    group.send(src, self.RB.at[u, h, k - 1], peers[k - 1])

        def b_finish(self, u, s):
            self.live["b", u].arrive()
            for h in range(2):
                _, _, j, _ = self.axes(h)
                total = self.CF[u, h, :, pl.ds(mult(j * 32, 32), 32), :]
                for k in range(3):
                    total = total + self.RB[u, h, k].astype(F32)
                self.PF[s, h] = total
                self.PB[s, h] = total.astype(BF)

        def y_start(self, s):
            group = self.live["y", s] = Group(self.RY.at[s])
            for h in range(2):
                for k in range(3):
                    group.send(self.PB.at[s, h], self.RY.at[s, h, k], ypeers[k])

        def y_finish(self, s):
            self.live["y", s].arrive()
            group = self.live["gb", s] = Group(RB2.at[0])
            for h in range(2):
                i, _, j, peers = self.axes(h)
                at = pl.ds(mult(j * 32, 32), 32)
                got = [self.RY[s, h, k].astype(F32) for k in range(3)]
                own = self.PF[s, h]
                if self.split:
                    self.G[s, Y, h * 4 + i, at, :] = (own + got[1])[0].astype(BF)
                    self.G[s, oY, h * 4 + i, at, :] = (got[0] + got[2])[0].astype(BF)
                else:
                    self.G[s, :, h * 4 + i, at, :] = (own + got[0] + (got[1] + got[2])).astype(BF)
                place = self.G.at[s, :, h * 4 + i, at, :]
                for to in peers:
                    group.send(place, place, to)

        def gb_finish(self, s):
            self.live["gb", s].arrive()

        def ga_start(self, s, key):
            group = self.live["ga", key] = Group(RA2.at[0])
            for h in range(2):
                i, peers, _, _ = self.axes(h)
                place = self.G.at[s, :, h * 4 + i]
                for to in peers:
                    group.send(place, place, to)

        def ga_finish(self, key):
            self.live["ga", key].arrive()

    first = Reduce((GF1, GP1, RA1, CB1, CF1, RB1, PB1, PF1, RY1, G1), True)
    second = Reduce((GF2, GP2, RA2, CB2, CF2, RB2, PB2, PF2, RY2, G2), False)

    def left(start, n, lanes):
        return WB[0, pl.ds(start, n), :, :, :, lanes].reshape(n * 128, -1)

    def right(s, lanes):
        return WB[1, 2 * s + c, :, :, :, lanes].reshape(128, -1)

    def middle(it, get):
        MID[it, 0] = jnp.zeros((8, 1536), F32)

        def body(n, _):
            lanes = pl.ds(mult(n * 512, 512), 512)
            for i in range(2):
                inner = jnp.dot(get(i), left(0, 4, lanes), preferred_element_type=F32)
                total = jnp.sum(inner[:128] * right(0, lanes).astype(F32), axis=0, keepdims=True)
                total = total + jnp.sum(
                    inner[128:] * right(1, lanes).astype(F32), axis=0, keepdims=True
                )
                MID[it, 0, pl.ds(i, 1), lanes] = total
            return 0

        lax.fori_loop(0, 3, body, 0)
        return one(MID.at[it, 0], MID.at[it, 1], core)

    def ladder(it, group):
        group.arrive()
        for i in range(2):
            for n in range(3):
                lanes = pl.ds(n * 512, 512)
                mid = MID[it, 0, i:i + 1, lanes] + MID[it, 1, i:i + 1, lanes]
                for s in range(2):
                    wr = right(s, lanes).astype(F32) * mid
                    WR[i, s * 128:(s + 1) * 128, lanes] = wr.astype(BF)

        def body(n, _):
            lf = left(n % 2 * 2, 2, pl.ds(0, 1536))
            LAD[pl.ds(mult(n * 256, 256), 256), :] = lax.dot_general(
                lf, WR[n // 2], NT, preferred_element_type=F32
            )
            return 0

        lax.fori_loop(0, 4, body, 0)

    def cycle(G, n, stages):
        here = pl.ds(mult(n * 256, 256), 256)
        mine = pl.ds(mult(Y * 1024 + n * 256, 256), 256)
        total = None
        for src, at, yy in ((BQ, mine, Y), (BR, here, oY)):
            for cc in range(2):
                blocks = [
                    jnp.concatenate([G[s, yy, cc * 4 + q] for q in range(4)], axis=1)
                    for s in stages
                ]
                weight = blocks[0] if len(blocks) == 1 else jnp.concatenate(blocks, axis=0)
                term = lax.dot_general(src[cc, at, :], weight, NT, preferred_element_type=F32)
                total = term if total is None else total + term
        return here, total

    def finish(n, here, s, lad, total):
        va = VA[pl.ds(mult(n % 2 * 256, 256), 256), :]
        vb = vir[0:1, pl.ds(mult((2 * s + c) * 128, 128), 128)]
        denom = va + vb - occ[2 * Y + n // 2] - piv[0]
        return ((C[s, here, :].astype(F32) + (total + lad)) / denom).astype(BF)

    b_in.arrive()
    gram1(0, Y, oc, 0)
    gram1(0, Y, oc, 1)
    for h in range(2):
        first.a_start(0, h)
    for copy in lcopies[2:]:
        copy.wait()
    thc_y.arrive()
    wide = WB.at[0, 0, :, pl.ds(0, 3), :, pl.ds(0, 768)]
    lx = to_all(WB.at[0, z, :, x, :, plane], WB.at[0, z, :, x, :, plane], xpeers, wide)
    rz = to_all(WB.at[1, z, :, x, :, plane], WB.at[1, z, :, x, :, plane], zpeers, wide)
    first.a_finish(0)
    lx.arrive()
    rz.arrive()
    thc = []

    def spread(part):
        lanes = pl.ds(mult(c * 768 + part * 384, 128), 384)
        ruler = WB.at[0, pl.ds(0, 3), :, :, :, pl.ds(0, 384)]
        src = WB.at[0, z, :, :, :, lanes]
        thc.append(to_all(src, src, zpeers, ruler))
        src = WB.at[1, :, :, x, :, lanes]
        thc.append(to_all(src, src, xpeers, ruler))

    spread(0)
    first.b_finish(0, Y)
    move(EARLY)
    for half in range(2):
        t_in[half].arrive()
        transpose0(oY, half)
        gram1(1, oY, 0, half)
        if half == 1:
            first.a_start(1, 0)
        gram1(1, oY, 1, half)
    first.a_start(1, 1)
    first.a_finish(1)
    spread(1)
    first.b_finish(1, oY)
    for s in range(2):
        first.y_start(s)
    move(N_MOVE - EARLY)
    for group in thc:
        group.arrive()
    thc_core = [one(WB.at[0, :, :, :, :, plane], WB.at[0, :, :, :, :, plane], core)]
    group = Group(WB.at[1, pl.ds(0, 2), :, :, :, pl.ds(0, 768)])
    for k in range(2):
        place = WB.at[1, oc + 2 * k, :, :, :, plane]
        group.send(place, place, core)
    thc_core.append(group)
    for s in range(2):
        first.y_finish(s)
    for group in thc_core:
        group.arrive()
    mid = middle(0, lambda i: TT0[:, :, pl.ds(mult(rows + i * 512, 512), 512)].reshape(256, 512))
    for s in range(2):
        first.gb_finish(s)
        first.ga_start(s, s)
    ladder(0, mid)
    forward(N_MOVE // 2)
    for s in range(2):
        first.ga_finish(s)
    for group in forwarded:
        group.arrive()

    def update1(n, _):
        here, total = cycle(G1, n, (0, 1))
        for s in range(2):
            at = slice(s * 128, (s + 1) * 128)
            value = finish(n, here, s, LAD[here, at], total[:, at])
            TT1[s, :, here] = jnp.transpose(value)
        return 0

    lax.fori_loop(0, 4, update1, 0)

    for cc in range(2):
        for src, at, yy in ((BQ, pl.ds(rows, 1024), Y), (BR, pl.ds(0, 1024), oY)):
            got = jnp.dot(
                TT1[...].reshape(256, 1024), src[cc, at, :], preferred_element_type=F32
            )
            for s in range(2):
                for q in range(4):
                    value = got[s * 128:(s + 1) * 128, q * 128:(q + 1) * 128]
                    GF2[s, yy, cc * 4 + q] = value
                    GP2[s, yy, cc * 4 + q] = value.astype(BF)
        for s in range(2):
            second.a_start(s, cc)
    mid = middle(1, lambda i: TT1[:, :, pl.ds(i * 512, 512)].reshape(256, 512))
    ladder(1, mid)
    for s in range(2):
        second.a_finish(s)
    for s in range(2):
        second.b_finish(s, s)
        second.y_start(s)
    for s in range(2):
        second.y_finish(s)
    for s in range(2):
        second.gb_finish(s)
    second.ga_start(oY, 0)
    second.ga_start(Y, 1)

    second.ga_finish(0)
    last = Group(TS)
    for n in range(4):
        here, total = cycle(G2, n, (oY,))
        lad = LAD[here, pl.ds(mult(oY * 128, 128), 128)]
        TS[here, :] = finish(n, here, oY, lad, total)
        last.send(TS.at[here, :], out.at[pl.ds(mult(Y * 1024 + n * 256, 256), 256), :], ypeers[0])
    second.ga_finish(1)

    def update2(n, _):
        here, total = cycle(G2, n, (Y,))
        lad = LAD[here, pl.ds(mult(Y * 128, 128), 128)]
        out[pl.ds(mult(Y * 1024 + n * 256, 256), 256), :] = finish(n, here, Y, lad, total)
        return 0

    lax.fori_loop(0, 4, update2, 0)
    last.arrive()
    for group in groups:
        group.sent()


def per_device(amplitudes, coulomb, df_factors, thc_left, thc_right, occ, vir, pivot):
    any_ = pl.BlockSpec(memory_space=pl.ANY)
    smem = pl.BlockSpec(memory_space=pltpu.SMEM)
    vmem = pl.BlockSpec(memory_space=pltpu.VMEM)

    def reduce_scratch(m):
        return [
            pltpu.VMEM((2, m, 8, 128, 128), F32),
            pltpu.VMEM((2, m, 8, 128, 128), BF),
            pltpu.VMEM((2, 2, 3, m, 128, 128), BF),
            pltpu.VMEM((2, 2, m, 128, 128), BF),
            pltpu.VMEM((2, 2, m, 128, 128), F32),
            pltpu.VMEM((2, 2, 3, m, 32, 128), BF),
            pltpu.VMEM((2, 2, m, 32, 128), BF),
            pltpu.VMEM((2, 2, m, 32, 128), F32),
            pltpu.VMEM((2, 2, 3, m, 32, 128), BF),
            pltpu.VMEM((2, 2, 8, 128, 128), BF),
        ]

    return pl.pallas_call(
        kernel,
        out_shape=jax.ShapeDtypeStruct((2048, 128), BF),
        in_specs=[any_] * 5 + [smem, vmem, smem],
        out_specs=vmem,
        scratch_shapes=[
            pltpu.VMEM((2, 2048, 512), BF),
            pltpu.VMEM((2, 1024, 512), BF),
            pltpu.VMEM((2, 2048, 128), BF),
            pltpu.VMEM((2, 128, 2048), BF),
            pltpu.VMEM((2, 128, 1024), BF),
            pltpu.VMEM((1024, 128), BF),
            pltpu.VMEM((2, 1024, 128), BF),
            pltpu.VMEM((1024, 256), F32),
            pltpu.VMEM((512, 128), F32),
            pltpu.VMEM((2, 4, 2, 4, 16, 1536), BF),
            pltpu.VMEM((2, 256, 1536), BF),
            pltpu.VMEM((2, 2, 8, 1536), F32),
        ]
        + reduce_scratch(1)
        + reduce_scratch(2)
        + [
            pltpu.SemaphoreType.DMA((N_SEM,)),
            pltpu.SemaphoreType.DMA((N_SEM,)),
            pltpu.SemaphoreType.DMA((6,)),
        ],
        compiler_params=pltpu.CompilerParams(
            collective_id=0, has_side_effects=True, vmem_limit_bytes=56 * 2**20
        ),
    )(amplitudes, coulomb, df_factors, thc_left, thc_right, occ, vir.reshape(1, 512), pivot)


def solution(mesh):
    in_specs = (
        P("pair", "aux"),
        P("pair", None),
        P("pair", "aux"),
        P("pair", "aux"),
        P("pair", "aux"),
        P("pair"),
        P(),
        P(),
    )
    return jax.shard_map(
        per_device, mesh=mesh, in_specs=in_specs, out_specs=P("pair", "aux"), check_vma=False
    )
```

time: 728 us -> 86.7 us (0.12)
  blocking collectives: 572 us -> 0 us
  waiting for transfers between devices: 101 us -> 0 us
  Pallas kernels: 0 us -> 84 us
  matrix products: 20.9 us -> 0 us
  between operations: 13.9 us -> 0.66 us
  local copies, waits for them, and re-layouts: 9.74 us -> 1.87 us
  other arithmetic: 7.65 us -> 0 us
    psum x2 -> x0, blocking collectives: 385 us -> none  [per_device(): gram = lax.psum(gram, 'pair').astype(jnp.bfloat16)]
    all_gather x2 -> x0, blocking collectives: 187 us -> none  [the longest x1 97.8 us: per_device(): lax.all_gather(thc_left, 'pair', axis=0, tiled=True)]
    pallas_call x0 -> x1, Pallas kernels: none -> 84 us  [per_device(): pl.pallas_call(kernel, out_shape=jax.ShapeDtypeStruct((2048, 128), BF), i...]
    reduce_scatter x2 -> x0, waiting for transfers between devices: 70.3 us -> none  [per_device(): share = lax.psum_scatter(part, 'aux', scatter_dimension=1, tiled=True)]
    all_gather x2 -> x0, waiting for transfers between devices: 29.8 us -> none  [per_device(): whole = lax.all_gather(local, 'aux', axis=1, tiled=True)]
    dot_general x8 -> x0, matrix products: 20.9 us -> none  [the longest x2 6.62 us: per_device(): lax.dot_general(weighted, right, (((1,), (1,)), ((), ())), preferred_elem...]
    convert_element_type x5 -> x0, other arithmetic: 7.52 us -> none  [the longest x2 4.51 us: per_device(): ((coulomb_block.astype(jnp.float32) + share) / denom_block).astype(jnp.bf...]
  transfers between devices with their start and end apart: 4 -> 0, of which waited for: 3 -> 0; matrix products, arithmetic and copies ran while one was open for 1% -> 0% of each run, Pallas kernels for 0% -> 0%
where the time goes in v2:
time: 86.7 us; the launch traced here: 86.5 us
  Pallas kernels  84 us (97%)
  local copies, waits for them, and re-layouts  1.87 us (2%)
    pallas_call x1, Pallas kernels, per_device(): pl.pallas_call(kernel, out_shape=jax.ShapeDtypeStruct((2048, 128), BF), i...  84 us
    unnamed x1, local copies, waits for them, and re-layouts  1.87 us

profile of v2, /device:TPU:8, one launch (start us, length us, event | category | flops | bytes accessed | tf_op | source)
XLA Modules:
  0.0 86.5 jit_solution(13939352108738397912)
XLA Ops:
  0.7 84.0 %shard_map.82 = bf16[2048,128]{1,0:T(8,128)(2,1)} custom-call(bf16[2048,128]{1,0:T(8,128)(2,1)} %amps.1, bf16[2048,512]{1,0:T(8,128)(2,1)} %coul.1, bf16[2048,512]{1,0:T(8,128)(2,1)} %df.1, bf16[16,384]{1,0:T(8,128)(2,1)} %tl.1, bf16[16,384]{1,0:T(8,128)(2,1)} %tr.1, f32[4]{0:T(128)} %occ.1, f32[1,512]{1,0:T(1,128)} %bitcast.1, f32[1]{0:T(128)S(6)} %copy.10.piv), custom_call_target="tpu_custom_call" | custom-call | tf_op jit(solution)/shard_map/pallas_call | solution.py:436
  84.7 1.9 %copy.11 = bf16[2048,128]{1,0:T(8,128)(2,1)} copy(bf16[2048,128]{1,0:T(8,128)(2,1)} %shard_map.82) | data formatting | bytes 1048576

commit v3 on v2

v3 whole, which is shorter than its diff:
```python
import jax
import jax.numpy as jnp
from jax import lax
from jax.experimental import pallas as pl
from jax.experimental.pallas import tpu as pltpu
from jax.sharding import PartitionSpec as P

MESH = pl.DeviceIdType.MESH
BF = jnp.bfloat16
F32 = jnp.float32
N_SEM = 57
N_MOVE = 8
EARLY = 4
NT = (((1,), (1,)), ((), ()))


def mult(value, n):
    return pl.multiple_of(value, n)


def kernel(
    amps, coul, df, tl, tr, occ, vir, piv, out,
    BQ, BR, T0, TT0, TT1, T1, TS, C, LAD, VA, WB, WR, MID,
    GF1, GP1, RA1, CB1, CF1, RB1, PB1, PF1, RY1, G1,
    GF2, GP2, RA2, CB2, CF2, RB2, PB2, PF2, RY2, G2,
    ss, rs, ls,
):
    a = lax.axis_index("aux")
    p = lax.axis_index("pair")
    Y, c = a // 2, a % 2
    z, yh, x = p // 8, (p // 4) % 2, p % 4
    oY, oc, oyh = 1 - Y, 1 - c, 1 - yh

    def dev(Y=Y, c=c, z=z, yh=yh, x=x):
        return {"aux": Y * 2 + c, "pair": z * 8 + yh * 4 + x}

    ypeers = [dev(Y=oY), dev(yh=oyh), dev(Y=oY, yh=oyh)]
    yring = [dev(Y=(yh * 2 + Y + k) % 2, yh=(yh * 2 + Y + k) % 4 // 2) for k in (1, 2, 3)]
    xpeers = [dev(x=(x + k) % 4) for k in (1, 2, 3)]
    zpeers = [dev(z=(z + k) % 4) for k in (1, 2, 3)]
    core = dev(c=oc)
    blocks = [c, 1 - c]
    rows = mult(Y * 1024, 1024)
    orows = mult(oY * 1024, 1024)

    count = [0]
    groups = []

    class Group:
        def __init__(self, ruler):
            self.n, self.ruler = count[0], ruler
            count[0] += 1
            assert self.n < N_SEM
            groups.append(self)

        def send(self, src, dst, to):
            pltpu.make_async_remote_copy(
                src_ref=src, dst_ref=dst, send_sem=ss.at[self.n], recv_sem=rs.at[self.n],
                device_id=to, device_id_type=MESH,
            ).start()

        def arrive(self):
            pltpu.make_async_copy(self.ruler, self.ruler, rs.at[self.n]).wait()

        def sent(self):
            pltpu.make_async_copy(self.ruler, self.ruler, ss.at[self.n]).wait()

    def one(src, dst, to):
        group = Group(dst)
        group.send(src, dst, to)
        return group

    def to_all(src, dst, peers, ruler):
        group = Group(ruler)
        for to in peers:
            group.send(src, dst, to)
        return group

    piece = pl.ds(mult(c * 768 + Y * 384, 128), 384)
    plane = pl.ds(mult(c * 768, 128), 768)
    lcopies = []
    for n, (src, dst) in enumerate([
        (amps, T0.at[Y]),
        (df, BQ.at[c]),
        (tl, WB.at[0, z, yh, x, :, piece]),
        (tr, WB.at[1, z, yh, x, :, piece]),
        (coul.at[pl.ds(rows, 1024), pl.ds(mult((2 * blocks[0] + c) * 128, 128), 128)], C.at[0]),
        (coul.at[pl.ds(rows, 1024), pl.ds(mult((2 * blocks[1] + c) * 128, 128), 128)], C.at[1]),
    ]):
        copy = pltpu.make_async_copy(src, dst, ls.at[n])
        copy.start()
        lcopies.append(copy)

    barrier = pltpu.get_barrier_semaphore()
    for to in ypeers + xpeers + zpeers + [core]:
        pl.semaphore_signal(barrier, inc=1, device_id=to, device_id_type=MESH)

    def transpose0(s, half):
        for n in range(2):
            at = pl.ds(half * 1024 + n * 512, 512)
            TT0[s, :, at] = jnp.transpose(T0[s, at, :])

    def gram1(f, s, cc, half):
        at = pl.ds(half * 1024, 1024)
        got = jnp.dot(TT0[s, :, at], BQ[cc, at, :], preferred_element_type=F32)
        for q in range(4):
            value = got[:, q * 128:(q + 1) * 128]
            if half == 1:
                value = GF1[f, 0, cc * 4 + q] + value
                GP1[f, 0, cc * 4 + q] = value.astype(BF)
            GF1[f, 0, cc * 4 + q] = value

    pl.semaphore_wait(barrier, 10)

    b_in = one(df, BQ.at[c], core)
    thc_y = Group(WB.at[0, 0, 0, pl.ds(0, 2), :, pl.ds(0, 1152)])
    for to in ypeers:
        thc_y.send(tl, WB.at[0, z, yh, x, :, piece], to)
        thc_y.send(tr, WB.at[1, z, yh, x, :, piece], to)
    t_in = []
    for half in range(2):
        at = pl.ds(half * 1024, 1024)
        t_in.append(one(amps.at[at, :], T0.at[Y, at, :], ypeers[0]))

    lcopies[0].wait()
    transpose0(Y, 0)
    transpose0(Y, 1)
    for q in range(4):
        row = vir[0:1, q * 128:(q + 1) * 128]
        VA[q * 128:(q + 1) * 128, :] = jnp.transpose(jnp.broadcast_to(row, (128, 128)))
    lcopies[1].wait()
    gram1(0, Y, c, 0)
    gram1(0, Y, c, 1)

    size = 1024 // N_MOVE
    moved = [Group(BR.at[0, pl.ds(n * size, size), :]) for n in range(N_MOVE)]

    def move(start, stop):
        for n in range(start, stop):
            src = df.at[pl.ds(mult(oY * 1024 + n * size, size), size), :]
            moved[n].send(src, BR.at[c, pl.ds(n * size, size), :], ypeers[0])

    forwarded = []

    def forward(count):
        start = len(forwarded) * 2
        for n in range(start, start + count * 2, 2):
            moved[n].arrive()
            moved[n + 1].arrive()
            block = BR.at[c, pl.ds(n * size, 2 * size), :]
            forwarded.append(one(block, block, core))

    class Reduce:
        def __init__(self, refs, split, gb_ruler, ga_ruler):
            self.GF, self.GP, self.RA, self.CB, self.CF = refs[:5]
            self.RB, self.PB, self.PF, self.RY, self.G = refs[5:]
            self.split, self.gb_ruler, self.ga_ruler = split, gb_ruler, ga_ruler
            self.part = self.GP.shape[3] // 4
            self.live = {}

        def axes(self, u, h):
            if u == 3:
                return (yh * 2 + Y, yring) + ((x, xpeers, zpeers) if h == 0 else (z, zpeers, xpeers))
            return ((x, xpeers, z, zpeers) if h == 0 else (z, zpeers, x, xpeers)) + (ypeers,)

        def own(self, j):
            return pl.ds(mult(j * self.part, self.part), self.part)

        def a_start(self, u, h):
            i, peers, _, _, _ = self.axes(u, h)
            if ("a", u) not in self.live:
                self.live["a", u] = Group(self.RA.at[u])
            for k in (1, 2, 3):
                src = self.GP.at[u, :, h * 4 + (i + k) % 4]
                self.live["a", u].send(src, self.RA.at[u, h, k - 1], peers[k - 1])

        def a_finish(self, u):
            self.live["a", u].arrive()
            group = self.live["b", u] = Group(self.RB.at[u])
            for h in range(2):
                i, _, j, peers, _ = self.axes(u, h)
                total = self.GF[u, :, h * 4 + i]
                for k in range(3):
                    total = total + self.RA[u, h, k].astype(F32)
                self.CF[u, h] = total
                self.CB[u, h] = total.astype(BF)
                for k in (1, 2, 3):
                    src = self.CB.at[u, h, :, self.own((j + k) % 4), :]
                    group.send(src, self.RB.at[u, h, k - 1], peers[k - 1])

        def b_finish(self, u, s):
            self.live["b", u].arrive()
            for h in range(2):
                _, _, j, _, _ = self.axes(u, h)
                total = self.CF[u, h, :, self.own(j), :]
                for k in range(3):
                    total = total + self.RB[u, h, k].astype(F32)
                self.PF[s, h] = total
                self.PB[s, h] = total.astype(BF)

        def y_start(self, s):
            group = self.live["y", s] = Group(self.RY.at[s])
            for h in range(2):
                peers = ypeers if self.split else self.axes(s, h)[4]
                for k in range(3):
                    group.send(self.PB.at[s, h], self.RY.at[s, h, k], peers[k])

        def y_finish(self, s):
            self.live["y", s].arrive()
            group = self.live["gb", s] = Group(self.gb_ruler)
            for h in range(2):
                i, _, j, peers, _ = self.axes(s, h)
                at = self.own(j)
                got = [self.RY[s, h, k].astype(F32) for k in range(3)]
                own = self.PF[s, h]
                if self.split:
                    self.G[s, Y, h * 4 + i, at, :] = (own + got[1])[0].astype(BF)
                    self.G[s, oY, h * 4 + i, at, :] = (got[0] + got[2])[0].astype(BF)
                else:
                    self.G[s, :, h * 4 + i, at, :] = (own + got[0] + (got[1] + got[2])).astype(BF)
                place = self.G.at[s, :, h * 4 + i, at, :]
                for to in peers:
                    group.send(place, place, to)

        def gb_finish(self, s):
            self.live["gb", s].arrive()
            group = self.live["ga", s] = Group(self.ga_ruler)
            for h in range(2):
                i, peers, _, _, _ = self.axes(s, h)
                place = self.G.at[s, :, h * 4 + i]
                for to in peers:
                    group.send(place, place, to)

        def ga_finish(self, s):
            self.live["ga", s].arrive()

    first = Reduce(
        (GF1, GP1, RA1, CB1, CF1, RB1, PB1, PF1, RY1, G1), True, RA1.at[0, 0], RA1
    )
    second = Reduce(
        (GF2, GP2, RA2, CB2, CF2, RB2, PB2, PF2, RY2, G2), False, RB2.at[0], RA2.at[0]
    )

    def left(start, n, lanes):
        return WB[0, pl.ds(start, n), :, :, :, lanes].reshape(n * 128, -1)

    def right(s, lanes):
        return WB[1, 2 * s + c, :, :, :, lanes].reshape(128, -1)

    def middle(it, i, order, inner_of):
        def body(n, _):
            lanes = pl.ds(mult(n * 512, 512), 512)
            inner = jnp.dot(inner_of, left(0, 4, lanes), preferred_element_type=F32)
            total = jnp.sum(inner[:128] * right(order[0], lanes).astype(F32), axis=0, keepdims=True)
            total = total + jnp.sum(
                inner[128:] * right(order[1], lanes).astype(F32), axis=0, keepdims=True
            )
            MID[it, 0, i:i + 1, lanes] = total
            return 0

        lax.fori_loop(0, 3, body, 0)

    def share(it):
        return one(MID.at[it, 0], MID.at[it, 1], core)

    def ladder_weights(it, group):
        group.arrive()
        for i in range(2):
            for n in range(3):
                lanes = pl.ds(n * 512, 512)
                mid = MID[it, 0, i:i + 1, lanes] + MID[it, 1, i:i + 1, lanes]
                for k in range(2):
                    wr = right(blocks[k], lanes).astype(F32) * mid
                    WR[i, k * 128:(k + 1) * 128, lanes] = wr.astype(BF)

    def ladder(start, stop):
        def body(n, _):
            lf = left(n % 2 * 2, 2, pl.ds(0, 1536))
            LAD[pl.ds(mult(n * 256, 256), 256), :] = lax.dot_general(
                lf, WR[n // 2], NT, preferred_element_type=F32
            )
            return 0

        lax.fori_loop(start, stop, body, 0)

    def cycle(G, n, stages):
        here = pl.ds(mult(n * 256, 256), 256)
        mine = pl.ds(mult(Y * 1024 + n * 256, 256), 256)
        total = None
        for src, at, yy in ((BQ, mine, Y), (BR, here, oY)):
            for cc in range(2):
                weight = jnp.concatenate(
                    [
                        jnp.concatenate([G[s, yy, cc * 4 + q] for q in range(4)], axis=1)
                        for s in stages
                    ],
                    axis=0,
                )
                term = lax.dot_general(src[cc, at, :], weight, NT, preferred_element_type=F32)
                total = term if total is None else total + term
        return here, total

    def finish(n, here, k, total):
        va = VA[pl.ds(mult(n % 2 * 256, 256), 256), :]
        vb = vir[0:1, pl.ds(mult((2 * blocks[k] + c) * 128, 128), 128)]
        denom = va + vb - occ[2 * Y + n // 2] - piv[0]
        lad = LAD[here, k * 128:(k + 1) * 128]
        return ((C[k, here, :].astype(F32) + (total + lad)) / denom).astype(BF)

    b_in.arrive()
    gram1(0, Y, oc, 0)
    gram1(0, Y, oc, 1)
    for copy in lcopies[2:]:
        copy.wait()
    thc_y.arrive()
    wide = WB.at[0, 0, :, pl.ds(0, 3), :, pl.ds(0, 768)]
    lx = to_all(WB.at[0, z, :, x, :, plane], WB.at[0, z, :, x, :, plane], xpeers, wide)
    rz = to_all(WB.at[1, z, :, x, :, plane], WB.at[1, z, :, x, :, plane], zpeers, wide)
    for h in range(2):
        first.a_start(0, h)
    lx.arrive()
    rz.arrive()
    third = WB.at[0, pl.ds(0, 3), :, :, :, pl.ds(0, 384)]

    def spread(part, pair):
        lanes = pl.ds(mult(c * 768 + part * 384, 128), 384)
        for to in range(3):
            src = WB.at[0, z, :, :, :, lanes]
            pair[0].send(src, src, zpeers[to])
            src = WB.at[1, :, :, x, :, lanes]
            pair[1].send(src, src, xpeers[to])

    soon = [Group(third), Group(third)]
    spread(0, soon)
    first.a_finish(0)
    for half in range(2):
        t_in[half].arrive()
        transpose0(oY, half)
        gram1(1, oY, 0, half)
        if half == 0:
            move(0, EARLY)
        else:
            first.a_start(1, 0)
        gram1(1, oY, 1, half)
    first.a_start(1, 1)
    late = [Group(third), Group(third)]
    spread(1, late)
    first.b_finish(0, (Y + c) % 2)
    first.a_finish(1)
    first.b_finish(1, (oY + c) % 2)
    for k in range(2):
        first.y_start(k)

    @pl.when(c == 0)
    def _():
        move(EARLY, N_MOVE)

    for group in soon + late:
        group.arrive()
    thc_core = [one(WB.at[0, :, :, :, :, plane], WB.at[0, :, :, :, :, plane], core)]
    group = Group(WB.at[1, pl.ds(0, 2), :, :, :, pl.ds(0, 768)])
    for k in range(2):
        place = WB.at[1, oc + 2 * k, :, :, :, plane]
        group.send(place, place, core)
    thc_core.append(group)
    for k in range(2):
        first.y_finish(k)
    for k in range(2):
        first.gb_finish(k)

    @pl.when(c == 1)
    def _():
        move(EARLY, N_MOVE)

    for group in thc_core:
        group.arrive()
    MID[0, 0] = jnp.zeros((8, 1536), F32)
    MID[1, 0] = jnp.zeros((8, 1536), F32)
    for i in range(2):
        at = pl.ds(mult(rows + i * 512, 512), 512)
        middle(0, i, (0, 1), TT0[:, :, at].reshape(256, 512))
    mid = share(0)
    forward(2)
    ladder_weights(0, mid)
    ladder(0, 4)
    forward(2)
    for k in range(2):
        first.ga_finish(k)

    def update1(n):
        here, total = cycle(G1, n, (0, 1))
        for k in range(2):
            value = finish(n, here, k, total[:, k * 128:(k + 1) * 128])
            TT1[k, :, here] = jnp.transpose(value)

    def first_rows(n, _):
        update1(n)
        return 0

    for group in forwarded:
        group.arrive()
    lax.fori_loop(0, 4, first_rows, 0)

    def gram2(cc):
        for src, at, yy in ((BQ, pl.ds(rows, 1024), Y), (BR, pl.ds(0, 1024), oY)):
            got = jnp.dot(
                TT1[...].reshape(256, 1024), src[cc, at, :], preferred_element_type=F32
            )
            for j in range(4):
                for q in range(4):
                    value = got[j * 64:(j + 1) * 64, q * 128:(q + 1) * 128]
                    GF2[j, yy, cc * 4 + q] = value
                    GP2[j, yy, cc * 4 + q] = value.astype(BF)
        for j in range(4):
            second.a_start(j, cc)

    gram2(0)
    gram2(1)

    for i in range(2):
        middle(1, i, blocks, TT1[:, :, i * 512:(i + 1) * 512].reshape(256, 512))
    mid = share(1)
    steps = [
        ("a", 0), ("a", 1), ("l", 0), ("a", 2), ("a", 3), ("l", 1), ("b", 0), ("b", 1), ("l", 2),
        ("b", 2), ("l", 3), ("b", 3), ("y", 0), ("y", 1), ("l", 4), ("y", 2), ("y", 3),
        ("g", 0), ("g", 1), ("g", 2), ("g", 3),
    ]
    for step, j in steps:
        if step == "l":
            if j == 0:
                ladder_weights(1, mid)
            else:
                ladder(j - 1, j)
        elif step == "a":
            second.a_finish(j)
        elif step == "b":
            second.b_finish(j, j)
            second.y_start(j)
        elif step == "y":
            second.y_finish(j)
        else:
            second.gb_finish(j)

    last = Group(TS)
    for k in range(2):
        second.ga_finish(2 * k)
        second.ga_finish(2 * k + 1)
        for n in range(4):
            here, total = cycle(G2, n, (2 * k, 2 * k + 1))
            value = finish(n, here, k, total)
            there = out.at[pl.ds(mult(Y * 1024 + n * 256, 256), 256), :]

            @pl.when(blocks[k] == oY)
            def _():
                TS[here, :] = value
                last.send(TS.at[here, :], there, ypeers[0])

            @pl.when(blocks[k] == Y)
            def _():
                T1[here, :] = value
                pltpu.make_async_copy(T1.at[here, :], there, ls.at[6]).start()

    pltpu.make_async_copy(T1, out.at[pl.ds(rows, 1024), :], ls.at[6]).wait()
    last.arrive()
    for group in groups:
        group.sent()


def per_device(amplitudes, coulomb, df_factors, thc_left, thc_right, occ, vir, pivot):
    any_ = pl.BlockSpec(memory_space=pl.ANY)
    smem = pl.BlockSpec(memory_space=pltpu.SMEM)
    vmem = pl.BlockSpec(memory_space=pltpu.VMEM)

    def reduce_scratch(n, m, b):
        return [
            pltpu.VMEM((n, m, 8, b, 128), F32),
            pltpu.VMEM((n, m, 8, b, 128), BF),
            pltpu.VMEM((n, 2, 3, m, b, 128), BF),
            pltpu.VMEM((n, 2, m, b, 128), BF),
            pltpu.VMEM((n, 2, m, b, 128), F32),
            pltpu.VMEM((n, 2, 3, m, b // 4, 128), BF),
            pltpu.VMEM((n, 2, m, b // 4, 128), BF),
            pltpu.VMEM((n, 2, m, b // 4, 128), F32),
            pltpu.VMEM((n, 2, 3, m, b // 4, 128), BF),
            pltpu.VMEM((n, 2, 8, b, 128), BF),
        ]

    return pl.pallas_call(
        kernel,
        out_shape=jax.ShapeDtypeStruct((2048, 128), BF),
        in_specs=[any_] * 5 + [smem, vmem, smem],
        out_specs=any_,
        scratch_shapes=[
            pltpu.VMEM((2, 2048, 512), BF),
            pltpu.VMEM((2, 1024, 512), BF),
            pltpu.VMEM((2, 2048, 128), BF),
            pltpu.VMEM((2, 128, 2048), BF),
            pltpu.VMEM((2, 128, 1024), BF),
            pltpu.VMEM((1024, 128), BF),
            pltpu.VMEM((1024, 128), BF),
            pltpu.VMEM((2, 1024, 128), BF),
            pltpu.VMEM((1024, 256), F32),
            pltpu.VMEM((512, 128), F32),
            pltpu.VMEM((2, 4, 2, 4, 16, 1536), BF),
            pltpu.VMEM((2, 256, 1536), BF),
            pltpu.VMEM((2, 2, 8, 1536), F32),
        ]
        + reduce_scratch(2, 1, 128)
        + reduce_scratch(4, 2, 64)
        + [
            pltpu.SemaphoreType.DMA((N_SEM,)),
            pltpu.SemaphoreType.DMA((N_SEM,)),
            pltpu.SemaphoreType.DMA((7,)),
        ],
        compiler_params=pltpu.CompilerParams(
            collective_id=0, has_side_effects=True, vmem_limit_bytes=56 * 2**20
        ),
    )(amplitudes, coulomb, df_factors, thc_left, thc_right, occ, vir.reshape(1, 512), pivot)


def solution(mesh):
    in_specs = (
        P("pair", "aux"),
        P("pair", None),
        P("pair", "aux"),
        P("pair", "aux"),
        P("pair", "aux"),
        P("pair"),
        P(),
        P(),
    )
    return jax.shard_map(
        per_device, mesh=mesh, in_specs=in_specs, out_specs=P("pair", "aux"), check_vma=False
    )
```

time: 86.7 us -> 82.7 us (0.954)
  Pallas kernels: 84 us -> 80 us
    pallas_call x1, Pallas kernels: 84 us -> 80 us  [per_device(): pl.pallas_call(kernel, out_shape=jax.ShapeDtypeStruct((2048, 128), BF), i...]
where the time goes in v3:
time: 82.7 us; the launch traced here: 82.5 us
  Pallas kernels  80 us (97%)
  local copies, waits for them, and re-layouts  1.87 us (2%)
    pallas_call x1, Pallas kernels, per_device(): pl.pallas_call(kernel, out_shape=jax.ShapeDtypeStruct((2048, 128), BF), i...  80 us
    unnamed x1, local copies, waits for them, and re-layouts  1.87 us

profile of v3, /device:TPU:8, one launch (start us, length us, event | category | flops | bytes accessed | tf_op | source)
XLA Modules:
  0.0 82.5 jit_solution(12031427687119269310)
XLA Ops:
  0.7 80.0 %shard_map.82 = bf16[2048,128]{1,0:T(8,128)(2,1)} custom-call(bf16[2048,128]{1,0:T(8,128)(2,1)} %amps.1, bf16[2048,512]{1,0:T(8,128)(2,1)} %coul.1, bf16[2048,512]{1,0:T(8,128)(2,1)} %df.1, bf16[16,384]{1,0:T(8,128)(2,1)} %tl.1, bf16[16,384]{1,0:T(8,128)(2,1)} %tr.1, f32[4]{0:T(128)} %occ.1, f32[1,512]{1,0:T(1,128)} %bitcast.1, f32[1]{0:T(128)S(6)} %copy.10.piv), custom_call_target="tpu_custom_call" | custom-call | tf_op jit(solution)/shard_map/pallas_call | solution.py:488
  80.7 1.9 %copy.11 = bf16[2048,128]{1,0:T(8,128)(2,1)} copy(bf16[2048,128]{1,0:T(8,128)(2,1)} %shard_map.82) | data formatting | bytes 1048576

commit v4 on v3

--- a/solution.py
+++ b/solution.py
@@ -9,6 +9,7 @@
 BF = jnp.bfloat16
 F32 = jnp.float32
 N_SEM = 57
+N_SENT = 20
 N_MOVE = 8
 EARLY = 4
 NT = (((1,), (1,)), ((), ()))
@@ -19,11 +20,11 @@
 
 
 def kernel(
-    amps, coul, df, tl, tr, occ, vir, piv, out,
+    amps, coul, df, tl, tr, occ_in, vir_in, piv_in, out,
     BQ, BR, T0, TT0, TT1, T1, TS, C, LAD, VA, WB, WR, MID,
     GF1, GP1, RA1, CB1, CF1, RB1, PB1, PF1, RY1, G1,
     GF2, GP2, RA2, CB2, CF2, RB2, PB2, PF2, RY2, G2,
-    ss, rs, ls,
+    ss, rs, ls, occ, vir, piv,
 ):
     a = lax.axis_index("aux")
     p = lax.axis_index("pair")
@@ -44,34 +45,34 @@
     orows = mult(oY * 1024, 1024)
 
     count = [0]
-    groups = []
+    kinds = {}
 
     class Group:
-        def __init__(self, ruler):
+        def __init__(self, ruler, kind=None, total=None):
             self.n, self.ruler = count[0], ruler
             count[0] += 1
-            assert self.n < N_SEM
-            groups.append(self)
+            if kind not in kinds:
+                kind = kind or str(self.n)
+                kinds[kind] = len(kinds), ruler if total is None else total
+            self.m = kinds[kind][0]
+            assert self.n < N_SEM and self.m < N_SENT
 
         def send(self, src, dst, to):
             pltpu.make_async_remote_copy(
-                src_ref=src, dst_ref=dst, send_sem=ss.at[self.n], recv_sem=rs.at[self.n],
+                src_ref=src, dst_ref=dst, send_sem=ss.at[self.m], recv_sem=rs.at[self.n],
                 device_id=to, device_id_type=MESH,
             ).start()
 
         def arrive(self):
             pltpu.make_async_copy(self.ruler, self.ruler, rs.at[self.n]).wait()
 
-        def sent(self):
-            pltpu.make_async_copy(self.ruler, self.ruler, ss.at[self.n]).wait()
-
-    def one(src, dst, to):
-        group = Group(dst)
+    def one(src, dst, to, *kind):
+        group = Group(dst, *kind)
         group.send(src, dst, to)
         return group
 
-    def to_all(src, dst, peers, ruler):
-        group = Group(ruler)
+    def to_all(src, dst, peers, ruler, *kind):
+        group = Group(ruler, *kind)
         for to in peers:
             group.send(src, dst, to)
         return group
@@ -86,6 +87,9 @@
         (tr, WB.at[1, z, yh, x, :, piece]),
         (coul.at[pl.ds(rows, 1024), pl.ds(mult((2 * blocks[0] + c) * 128, 128), 128)], C.at[0]),
         (coul.at[pl.ds(rows, 1024), pl.ds(mult((2 * blocks[1] + c) * 128, 128), 128)], C.at[1]),
+        (vir_in, vir),
+        (occ_in, occ),
+        (piv_in, piv),
     ]):
         copy = pltpu.make_async_copy(src, dst, ls.at[n])
         copy.start()
@@ -120,11 +124,12 @@
     t_in = []
     for half in range(2):
         at = pl.ds(half * 1024, 1024)
-        t_in.append(one(amps.at[at, :], T0.at[Y, at, :], ypeers[0]))
+        t_in.append(one(amps.at[at, :], T0.at[Y, at, :], ypeers[0], "t", T0.at[0]))
 
     lcopies[0].wait()
     transpose0(Y, 0)
     transpose0(Y, 1)
+    lcopies[6].wait()
     for q in range(4):
         row = vir[0:1, q * 128:(q + 1) * 128]
         VA[q * 128:(q + 1) * 128, :] = jnp.transpose(jnp.broadcast_to(row, (128, 128)))
@@ -133,7 +138,7 @@
     gram1(0, Y, c, 1)
 
     size = 1024 // N_MOVE
-    moved = [Group(BR.at[0, pl.ds(n * size, size), :]) for n in range(N_MOVE)]
+    moved = [Group(BR.at[0, pl.ds(n * size, size), :], "move", BR.at[0]) for n in range(N_MOVE)]
 
     def move(start, stop):
         for n in range(start, stop):
@@ -148,10 +153,11 @@
             moved[n].arrive()
             moved[n + 1].arrive()
             block = BR.at[c, pl.ds(n * size, 2 * size), :]
-            forwarded.append(one(block, block, core))
+            forwarded.append(one(block, block, core, "forward", BR.at[0]))
 
     class Reduce:
-        def __init__(self, refs, split, gb_ruler, ga_ruler):
+        def __init__(self, name, refs, split, gb_ruler, gb_total, ga_ruler):
+            self.name, self.gb_total = name, gb_total
             self.GF, self.GP, self.RA, self.CB, self.CF = refs[:5]
             self.RB, self.PB, self.PF, self.RY, self.G = refs[5:]
             self.split, self.gb_ruler, self.ga_ruler = split, gb_ruler, ga_ruler
@@ -169,14 +175,14 @@
         def a_start(self, u, h):
             i, peers, _, _, _ = self.axes(u, h)
             if ("a", u) not in self.live:
-                self.live["a", u] = Group(self.RA.at[u])
+                self.live["a", u] = Group(self.RA.at[u], self.name + "a", self.RA)
             for k in (1, 2, 3):
                 src = self.GP.at[u, :, h * 4 + (i + k) % 4]
                 self.live["a", u].send(src, self.RA.at[u, h, k - 1], peers[k - 1])
 
         def a_finish(self, u):
             self.live["a", u].arrive()
-            group = self.live["b", u] = Group(self.RB.at[u])
+            group = self.live["b", u] = Group(self.RB.at[u], self.name + "b", self.RB)
             for h in range(2):
                 i, _, j, peers, _ = self.axes(u, h)
                 total = self.GF[u, :, h * 4 + i]
@@ -199,7 +205,7 @@
                 self.PB[s, h] = total.astype(BF)
 
         def y_start(self, s):
-            group = self.live["y", s] = Group(self.RY.at[s])
+            group = self.live["y", s] = Group(self.RY.at[s], self.name + "y", self.RY)
             for h in range(2):
                 peers = ypeers if self.split else self.axes(s, h)[4]
                 for k in range(3):
@@ -207,7 +213,7 @@
 
         def y_finish(self, s):
             self.live["y", s].arrive()
-            group = self.live["gb", s] = Group(self.gb_ruler)
+            group = self.live["gb", s] = Group(self.gb_ruler, self.name + "gb", self.gb_total)
             for h in range(2):
                 i, _, j, peers, _ = self.axes(s, h)
                 at = self.own(j)
@@ -224,7 +230,7 @@
 
         def gb_finish(self, s):
             self.live["gb", s].arrive()
-            group = self.live["ga", s] = Group(self.ga_ruler)
+            group = self.live["ga", s] = Group(self.ga_ruler, self.name + "ga", RA2)
             for h in range(2):
                 i, peers, _, _, _ = self.axes(s, h)
                 place = self.G.at[s, :, h * 4 + i]
@@ -235,10 +241,10 @@
             self.live["ga", s].arrive()
 
     first = Reduce(
-        (GF1, GP1, RA1, CB1, CF1, RB1, PB1, PF1, RY1, G1), True, RA1.at[0, 0], RA1
+        "f", (GF1, GP1, RA1, CB1, CF1, RB1, PB1, PF1, RY1, G1), True, RA1.at[0, 0], RA1.at[0], RA1
     )
     second = Reduce(
-        (GF2, GP2, RA2, CB2, CF2, RB2, PB2, PF2, RY2, G2), False, RB2.at[0], RA2.at[0]
+        "s", (GF2, GP2, RA2, CB2, CF2, RB2, PB2, PF2, RY2, G2), False, RB2.at[0], RB2, RA2.at[0]
     )
 
     def left(start, n, lanes):
@@ -261,7 +267,7 @@
         lax.fori_loop(0, 3, body, 0)
 
     def share(it):
-        return one(MID.at[it, 0], MID.at[it, 1], core)
+        return one(MID.at[it, 0], MID.at[it, 1], core, "mid", MID.at[0])
 
     def ladder_weights(it, group):
         group.arrive()
@@ -310,12 +316,12 @@
     b_in.arrive()
     gram1(0, Y, oc, 0)
     gram1(0, Y, oc, 1)
-    for copy in lcopies[2:]:
+    for copy in lcopies[2:6] + lcopies[7:]:
         copy.wait()
     thc_y.arrive()
     wide = WB.at[0, 0, :, pl.ds(0, 3), :, pl.ds(0, 768)]
-    lx = to_all(WB.at[0, z, :, x, :, plane], WB.at[0, z, :, x, :, plane], xpeers, wide)
-    rz = to_all(WB.at[1, z, :, x, :, plane], WB.at[1, z, :, x, :, plane], zpeers, wide)
+    lx = to_all(WB.at[0, z, :, x, :, plane], WB.at[0, z, :, x, :, plane], xpeers, wide, "near", WB.at[0, 0, :, pl.ds(0, 3)])
+    rz = to_all(WB.at[1, z, :, x, :, plane], WB.at[1, z, :, x, :, plane], zpeers, wide, "near")
     for h in range(2):
         first.a_start(0, h)
     lx.arrive()
@@ -330,7 +336,7 @@
             src = WB.at[1, :, :, x, :, lanes]
             pair[1].send(src, src, xpeers[to])
 
-    soon = [Group(third), Group(third)]
+    soon = [Group(third, "far", WB.at[0, pl.ds(0, 3)]), Group(third, "far")]
     spread(0, soon)
     first.a_finish(0)
     for half in range(2):
@@ -343,7 +349,7 @@
             first.a_start(1, 0)
         gram1(1, oY, 1, half)
     first.a_start(1, 1)
-    late = [Group(third), Group(third)]
+    late = [Group(third, "far"), Group(third, "far")]
     spread(1, late)
     first.b_finish(0, (Y + c) % 2)
     first.a_finish(1)
@@ -357,8 +363,9 @@
 
     for group in soon + late:
         group.arrive()
-    thc_core = [one(WB.at[0, :, :, :, :, plane], WB.at[0, :, :, :, :, plane], core)]
-    group = Group(WB.at[1, pl.ds(0, 2), :, :, :, pl.ds(0, 768)])
+    whole = WB.at[0, :, :, :, :, plane]
+    thc_core = [one(whole, whole, core, "core", WB.at[0, pl.ds(0, 3)])]
+    group = Group(WB.at[1, pl.ds(0, 2), :, :, :, pl.ds(0, 768)], "core")
     for k in range(2):
         place = WB.at[1, oc + 2 * k, :, :, :, plane]
         group.send(place, place, core)
@@ -421,16 +428,13 @@
         middle(1, i, blocks, TT1[:, :, i * 512:(i + 1) * 512].reshape(256, 512))
     mid = share(1)
     steps = [
-        ("a", 0), ("a", 1), ("l", 0), ("a", 2), ("a", 3), ("l", 1), ("b", 0), ("b", 1), ("l", 2),
-        ("b", 2), ("l", 3), ("b", 3), ("y", 0), ("y", 1), ("l", 4), ("y", 2), ("y", 3),
-        ("g", 0), ("g", 1), ("g", 2), ("g", 3),
+        ("a", 0), ("a", 1), ("a", 2), ("a", 3), ("b", 0), ("b", 1), ("b", 2), ("b", 3),
+        ("y", 0), ("y", 1), ("y", 2), ("y", 3), ("g", 0), ("g", 1), ("g", 2), ("g", 3), ("l", 0),
     ]
     for step, j in steps:
         if step == "l":
-            if j == 0:
-                ladder_weights(1, mid)
-            else:
-                ladder(j - 1, j)
+            ladder_weights(1, mid)
+            ladder(0, 4)
         elif step == "a":
             second.a_finish(j)
         elif step == "b":
@@ -458,18 +462,16 @@
             @pl.when(blocks[k] == Y)
             def _():
                 T1[here, :] = value
-                pltpu.make_async_copy(T1.at[here, :], there, ls.at[6]).start()
-
-    pltpu.make_async_copy(T1, out.at[pl.ds(rows, 1024), :], ls.at[6]).wait()
+                pltpu.make_async_copy(T1.at[here, :], there, ls.at[9]).start()
+
+    pltpu.make_async_copy(T1, out.at[pl.ds(rows, 1024), :], ls.at[9]).wait()
     last.arrive()
-    for group in groups:
-        group.sent()
+    for m, total in kinds.values():
+        pltpu.make_async_copy(total, total, ss.at[m]).wait()
 
 
 def per_device(amplitudes, coulomb, df_factors, thc_left, thc_right, occ, vir, pivot):
     any_ = pl.BlockSpec(memory_space=pl.ANY)
-    smem = pl.BlockSpec(memory_space=pltpu.SMEM)
-    vmem = pl.BlockSpec(memory_space=pltpu.VMEM)
 
     def reduce_scratch(n, m, b):
         return [
@@ -488,7 +490,7 @@
     return pl.pallas_call(
         kernel,
         out_shape=jax.ShapeDtypeStruct((2048, 128), BF),
-        in_specs=[any_] * 5 + [smem, vmem, smem],
+        in_specs=[any_] * 8,
         out_specs=any_,
         scratch_shapes=[
             pltpu.VMEM((2, 2048, 512), BF),
@@ -508,9 +510,12 @@
         + reduce_scratch(2, 1, 128)
         + reduce_scratch(4, 2, 64)
         + [
+            pltpu.SemaphoreType.DMA((N_SENT,)),
             pltpu.SemaphoreType.DMA((N_SEM,)),
-            pltpu.SemaphoreType.DMA((N_SEM,)),
-            pltpu.SemaphoreType.DMA((7,)),
+            pltpu.SemaphoreType.DMA((10,)),
+            pltpu.SMEM((4,), F32),
+            pltpu.VMEM((1, 512), F32),
+            pltpu.SMEM((1,), F32),
         ],
         compiler_params=pltpu.CompilerParams(
             collective_id=0, has_side_effects=True, vmem_limit_bytes=56 * 2**20

time: 82.7 us -> 81.5 us (0.985)
  Pallas kernels: 80 us -> 78.8 us
    pallas_call x1, Pallas kernels: 80 us -> 78.8 us  [per_device(): pl.pallas_call(kernel, out_shape=jax.ShapeDtypeStruct((2048, 128), BF), i...]
where the time goes in v4:
time: 81.5 us; the launch traced here: 81.4 us
  Pallas kernels  78.8 us (97%)
  local copies, waits for them, and re-layouts  1.87 us (2%)
    pallas_call x1, Pallas kernels, per_device(): pl.pallas_call(kernel, out_shape=jax.ShapeDtypeStruct((2048, 128), BF), i...  78.8 us
    unnamed x1, local copies, waits for them, and re-layouts  1.87 us

profile of v4, /device:TPU:8, one launch (start us, length us, event | category | flops | bytes accessed | tf_op | source)
XLA Modules:
  0.0 81.4 jit_solution(2177204361158289315)
XLA Ops:
  0.7 78.8 %shard_map.82 = bf16[2048,128]{1,0:T(8,128)(2,1)} custom-call(bf16[2048,128]{1,0:T(8,128)(2,1)} %amps.1, bf16[2048,512]{1,0:T(8,128)(2,1)} %coul.1, bf16[2048,512]{1,0:T(8,128)(2,1)} %df.1, bf16[16,384]{1,0:T(8,128)(2,1)} %tl.1, bf16[16,384]{1,0:T(8,128)(2,1)} %tr.1, f32[4]{0:T(128)} %occ_in.1, f32[1,512]{1,0:T(1,128)} %bitcast.1, f32[1]{0:T(128)S(6)} %copy.10.piv_in), custom_call_target="tpu_custom_call" | custom-call | tf_op jit(solution)/shard_map/pallas_call | solution.py:490
  79.5 1.9 %copy.11 = bf16[2048,128]{1,0:T(8,128)(2,1)} copy(bf16[2048,128]{1,0:T(8,128)(2,1)} %shard_map.82) | data formatting | bytes 1048576

commit v5 on v4

--- a/solution.py
+++ b/solution.py
@@ -289,9 +289,9 @@
 
         lax.fori_loop(start, stop, body, 0)
 
-    def cycle(G, n, stages):
-        here = pl.ds(mult(n * 256, 256), 256)
-        mine = pl.ds(mult(Y * 1024 + n * 256, 256), 256)
+    def cycle(G, n, stages, size=256):
+        here = pl.ds(mult(n * size, size), size)
+        mine = pl.ds(mult(Y * 1024 + n * size, size), size)
         total = None
         for src, at, yy in ((BQ, mine, Y), (BR, here, oY)):
             for cc in range(2):
@@ -306,10 +306,11 @@
                 total = term if total is None else total + term
         return here, total
 
-    def finish(n, here, k, total):
-        va = VA[pl.ds(mult(n % 2 * 256, 256), 256), :]
+    def finish(n, here, k, total, size=256):
+        per = 512 // size
+        va = VA[pl.ds(mult(n % per * size, size), size), :]
         vb = vir[0:1, pl.ds(mult((2 * blocks[k] + c) * 128, 128), 128)]
-        denom = va + vb - occ[2 * Y + n // 2] - piv[0]
+        denom = va + vb - occ[2 * Y + n // per] - piv[0]
         lad = LAD[here, k * 128:(k + 1) * 128]
         return ((C[k, here, :].astype(F32) + (total + lad)) / denom).astype(BF)
 
@@ -395,9 +396,9 @@
         first.ga_finish(k)
 
     def update1(n):
-        here, total = cycle(G1, n, (0, 1))
+        here, total = cycle(G1, n, (0, 1), 512)
         for k in range(2):
-            value = finish(n, here, k, total[:, k * 128:(k + 1) * 128])
+            value = finish(n, here, k, total[:, k * 128:(k + 1) * 128], 512)
             TT1[k, :, here] = jnp.transpose(value)
 
     def first_rows(n, _):
@@ -406,7 +407,7 @@
 
     for group in forwarded:
         group.arrive()
-    lax.fori_loop(0, 4, first_rows, 0)
+    lax.fori_loop(0, 2, first_rows, 0)
 
     def gram2(cc):
         for src, at, yy in ((BQ, pl.ds(rows, 1024), Y), (BR, pl.ds(0, 1024), oY)):
@@ -449,10 +450,10 @@
     for k in range(2):
         second.ga_finish(2 * k)
         second.ga_finish(2 * k + 1)
-        for n in range(4):
-            here, total = cycle(G2, n, (2 * k, 2 * k + 1))
-            value = finish(n, here, k, total)
-            there = out.at[pl.ds(mult(Y * 1024 + n * 256, 256), 256), :]
+        for n in range(8):
+            here, total = cycle(G2, n, (2 * k, 2 * k + 1), 128)
+            value = finish(n, here, k, total, 128)
+            there = out.at[pl.ds(mult(Y * 1024 + n * 128, 128), 128), :]
 
             @pl.when(blocks[k] == oY)
             def _():

time: 81.5 us -> 80.7 us (level)
    pallas_call x1, Pallas kernels: 78.8 us -> 78 us  [per_device(): pl.pallas_call(kernel, out_shape=jax.ShapeDtypeStruct((2048, 128), BF), i...]
where the time goes in v5:
time: 80.7 us; the launch traced here: 80.5 us
  Pallas kernels  78 us (97%)
  local copies, waits for them, and re-layouts  1.87 us (2%)
    pallas_call x1, Pallas kernels, per_device(): pl.pallas_call(kernel, out_shape=jax.ShapeDtypeStruct((2048, 128), BF), i...  78 us
    unnamed x1, local copies, waits for them, and re-layouts  1.87 us

profile of v5, /device:TPU:8, one launch (start us, length us, event | category | flops | bytes accessed | tf_op | source)
XLA Modules:
  0.0 80.5 jit_solution(15585107545726953496)
XLA Ops:
  0.7 78.0 %shard_map.82 = bf16[2048,128]{1,0:T(8,128)(2,1)} custom-call(bf16[2048,128]{1,0:T(8,128)(2,1)} %amps.1, bf16[2048,512]{1,0:T(8,128)(2,1)} %coul.1, bf16[2048,512]{1,0:T(8,128)(2,1)} %df.1, bf16[16,384]{1,0:T(8,128)(2,1)} %tl.1, bf16[16,384]{1,0:T(8,128)(2,1)} %tr.1, f32[4]{0:T(128)} %occ_in.1, f32[1,512]{1,0:T(1,128)} %bitcast.1, f32[1]{0:T(128)S(6)} %copy.10.piv_in), custom_call_target="tpu_custom_call" | custom-call | tf_op jit(solution)/shard_map/pallas_call | solution.py:491
  78.7 1.9 %copy.11 = bf16[2048,128]{1,0:T(8,128)(2,1)} copy(bf16[2048,128]{1,0:T(8,128)(2,1)} %shard_map.82) | data formatting | bytes 1048576

commit v6 on v5

--- a/solution.py
+++ b/solution.py
@@ -405,9 +405,10 @@
         update1(n)
         return 0
 
-    for group in forwarded:
-        group.arrive()
-    lax.fori_loop(0, 2, first_rows, 0)
+    for n in range(2):
+        for group in forwarded[2 * n:2 * n + 2]:
+            group.arrive()
+        lax.fori_loop(n, n + 1, first_rows, 0)
 
     def gram2(cc):
         for src, at, yy in ((BQ, pl.ds(rows, 1024), Y), (BR, pl.ds(0, 1024), oY)):

time: 80.7 us -> 81.5 us (level)
  no operation moved by 1% of the time
where the time goes in v6:
time: 81.5 us; the launch traced here: 81.3 us
  Pallas kernels  78.8 us (97%)
  local copies, waits for them, and re-layouts  1.87 us (2%)
    pallas_call x1, Pallas kernels, per_device(): pl.pallas_call(kernel, out_shape=jax.ShapeDtypeStruct((2048, 128), BF), i...  78.8 us
    unnamed x1, local copies, waits for them, and re-layouts  1.87 us

profile of v6, /device:TPU:8, one launch (start us, length us, event | category | flops | bytes accessed | tf_op | source)
XLA Modules:
  0.0 81.3 jit_solution(16073035291363753523)
XLA Ops:
  0.7 78.8 %shard_map.82 = bf16[2048,128]{1,0:T(8,128)(2,1)} custom-call(bf16[2048,128]{1,0:T(8,128)(2,1)} %amps.1, bf16[2048,512]{1,0:T(8,128)(2,1)} %coul.1, bf16[2048,512]{1,0:T(8,128)(2,1)} %df.1, bf16[16,384]{1,0:T(8,128)(2,1)} %tl.1, bf16[16,384]{1,0:T(8,128)(2,1)} %tr.1, f32[4]{0:T(128)} %occ_in.1, f32[1,512]{1,0:T(1,128)} %bitcast.1, f32[1]{0:T(128)S(6)} %copy.10.piv_in), custom_call_target="tpu_custom_call" | custom-call | tf_op jit(solution)/shard_map/pallas_call | solution.py:492
  79.4 1.9 %copy.11 = bf16[2048,128]{1,0:T(8,128)(2,1)} copy(bf16[2048,128]{1,0:T(8,128)(2,1)} %shard_map.82) | data formatting | bytes 1048576
